TPU v7x, 32 devices: a whole 2x2x4 slice. The times are simulated.
32 devices in a mesh: dp: 16 (over z, y, x), tensor: 2 (over core).
Axes of the slice: x: 2, y: 2, z: 4, core: 2. Of those that a mesh axis runs over, the one named last changes fastest.
Arguments:
- tokens: bfloat16 [32768, 768], P('dp'), may hold values from -6.25 to 6.25, as said below
- long_lengths: int32 [32], P('dp'), may hold values from 128 to 512, as said below
- short_lengths: int32 [64], P('dp'), may hold values from 64 to 256, as said below
- query_weight: bfloat16 [768, 768], P(None, 'tensor'), may hold values from -0.21875 to 0.21875
- query_bias: float32 [768], P('tensor'), may hold values from -3 to 3
- key_weight: bfloat16 [768, 768], P(None, 'tensor'), may hold values from -0.21875 to 0.21875
- value_weight: bfloat16 [768, 768], P(None, 'tensor'), may hold values from -0.21875 to 0.21875
- value_bias: float32 [768], P('tensor'), may hold values from -3 to 3
- output_weight: bfloat16 [768, 768], P('tensor'), may hold values from -0.875 to 0.875
- output_bias: float32 [768], replicated, may hold values from -3 to 3
- first_gain: float32 [768], replicated, may hold values from 0.25 to 1.75
- first_shift: float32 [768], replicated, may hold values from -3 to 3
- inner_weight: bfloat16 [768, 3072], P(None, 'tensor'), may hold values from -0.21875 to 0.21875
- inner_bias: float32 [3072], P('tensor'), may hold values from -3 to 3
- outer_weight: bfloat16 [3072, 768], P('tensor'), may hold values from -0.109375 to 0.109375
- outer_bias: float32 [768], replicated, may hold values from -3 to 3
- second_gain: float32 [768], replicated, may hold values from 0.25 to 1.75
- second_shift: float32 [768], replicated, may hold values from -3 to 3
- out_grad: bfloat16 [32768, 768], P('dp'), may hold values from -6 to 6
Outputs:
- block_out: bfloat16 [32768, 768], P('dp')
- tokens_grad: bfloat16 [32768, 768], P('dp')
- query_weight_grad: float32 [768, 768], P('dp', 'tensor')
- query_bias_grad: float32 [768], P('tensor')
- key_weight_grad: float32 [768, 768], P('dp', 'tensor')
- value_weight_grad: float32 [768, 768], P('dp', 'tensor')
- value_bias_grad: float32 [768], P('tensor')
- output_weight_grad: float32 [768, 768], P('tensor', 'dp')
- output_bias_grad: float32 [768], replicated
- first_gain_grad: float32 [768], replicated
- first_shift_grad: float32 [768], replicated
- inner_weight_grad: float32 [768, 3072], P('dp', 'tensor')
- inner_bias_grad: float32 [3072], P('tensor')
- outer_weight_grad: float32 [3072, 768], P('tensor', 'dp')
- outer_bias_grad: float32 [768], replicated
- second_gain_grad: float32 [768], replicated
- second_shift_grad: float32 [768], replicated
- residual_rms: float32 [], replicated
- attention_rms: float32 [], replicated
- feedforward_rms: float32 [], replicated
Inputs may be any that keep to these rules, and one draw needn't show every extreme that they name: `long_lengths`: the entry of a long-bucket sequence; its slot positions from this length on are padding. `short_lengths`: the entry of a short-bucket sequence; its slot positions from this length on are padding. `tokens`: activations of order one.
All inputs are finite; a program needn't handle non-finite values.
Results may differ from a plain program's by a relative error of at most 0.02.
Values may be sent and summed in bfloat16 or wider, within the bound.
No kernel may reach another device: no remote copies, remote signals or barrier semaphores. Data moves between devices by JAX's collectives and lax.ppermute only.
A program may use at most 192 MiB of HBM per device.

v0:
```python
import jax
import jax.numpy as jnp
from jax import lax
from jax.sharding import PartitionSpec as P

D = 768
HEAD_DIM = 64
LONG = 512
SHORT = 256


eps_norm = 1e-05
masked_score = -1e30
query_block = 512


def normalize(values):
    centered = values - jnp.mean(values, axis=-1, keepdims=True)
    inverse_dev = lax.rsqrt(jnp.mean(centered * centered, axis=-1, keepdims=True) + eps_norm)
    return (centered * inverse_dev, inverse_dev)


def norm_backward(scaled, normed, inverse_dev):
    centred_grad = scaled - jnp.mean(scaled, axis=-1, keepdims=True)
    return inverse_dev * (centred_grad - normed * jnp.mean(scaled * normed, axis=-1, keepdims=True))


def key_valid(lengths, key_count):
    return jnp.arange(key_count, dtype=jnp.int32)[None, :] < lengths[:, None]


def token_valid(long_lengths, short_lengths):
    first = key_valid(long_lengths, LONG).reshape(-1)
    second = key_valid(short_lengths, SHORT).reshape(-1)
    return jnp.concatenate([first, second]).astype(jnp.float32)


def block_scores(queries, key_rows, usable):
    raw = jnp.einsum("bqhe,bkhe->bhqk", queries, key_rows, preferred_element_type=jnp.float32)
    return jnp.where(usable[:, None, None, :], raw * HEAD_DIM ** (-0.5), masked_score)


def attend_forward(queries, key_rows, values, lengths):
    key_count = key_rows.shape[1]
    usable = key_valid(lengths, key_count)
    scores = block_scores(queries, key_rows, usable)
    maximum = jnp.max(scores, axis=-1, keepdims=True)
    powers = jnp.exp(scores - maximum)
    totals = jnp.sum(powers, axis=-1, keepdims=True)
    weights = (powers / totals).astype(jnp.bfloat16)
    pieces = [jnp.einsum("bhqk,bkhe->bqhe", weights, values, preferred_element_type=jnp.float32)]
    log_parts = [(maximum + jnp.log(totals))[..., 0]]
    return (jnp.concatenate(pieces, 1), jnp.concatenate(log_parts, 2))


def attend_backward(queries, key_rows, values, lengths, log_sums, context_grad):
    key_count = key_rows.shape[1]
    usable = key_valid(lengths, key_count)
    block_rows = min(key_count, query_block)
    scale = HEAD_DIM ** (-0.5)
    key_grad = jnp.zeros(key_rows.shape, jnp.float32)
    value_grad = jnp.zeros(values.shape, jnp.float32)
    scores = block_scores(queries, key_rows, usable)
    probs = jnp.exp(scores - log_sums[:, :, 0:block_rows, None])
    prob_low = probs.astype(jnp.bfloat16)
    value_grad = value_grad + jnp.einsum(
        "bhqk,bqhe->bkhe", prob_low, context_grad, preferred_element_type=jnp.float32
    )
    prob_grad = jnp.einsum(
        "bqhe,bkhe->bhqk", context_grad, values, preferred_element_type=jnp.float32
    )
    row_dot = jnp.sum(probs * prob_grad, axis=-1, keepdims=True)
    score_grad = (probs * (prob_grad - row_dot)).astype(jnp.bfloat16)
    query_parts = [
        jnp.einsum("bhqk,bkhe->bqhe", score_grad, key_rows, preferred_element_type=jnp.float32)
        * scale
    ]
    key_grad = (
        key_grad
        + jnp.einsum("bhqk,bqhe->bkhe", score_grad, queries, preferred_element_type=jnp.float32)
        * scale
    )
    return (jnp.concatenate(query_parts, 1), key_grad, value_grad)


def split_buckets(array, long_count, heads_here):
    long_rows = long_count * LONG
    first = array[:long_rows].reshape(long_count, LONG, heads_here, HEAD_DIM)
    second = array[long_rows:].reshape(-1, SHORT, heads_here, HEAD_DIM)
    return (first, second)


def join_buckets(first, second, heads_here):
    width = heads_here * HEAD_DIM
    return jnp.concatenate([first.reshape(-1, width), second.reshape(-1, width)], 0)


def run_forward(queries, key_rows, values, long_lengths, short_lengths):
    heads_here = queries.shape[1] // HEAD_DIM
    long_count = long_lengths.shape[0]
    query_long, query_short = split_buckets(queries, long_count, heads_here)
    key_long, key_short = split_buckets(key_rows, long_count, heads_here)
    value_long, value_short = split_buckets(values, long_count, heads_here)

    def one_long(entries):
        context, log_sums = attend_forward(
            entries[0][None], entries[1][None], entries[2][None], entries[3][None]
        )
        return (context[0], log_sums[0])

    long_context, long_logs = lax.map(one_long, (query_long, key_long, value_long, long_lengths))
    short_context, short_logs = attend_forward(query_short, key_short, value_short, short_lengths)
    return (join_buckets(long_context, short_context, heads_here), (long_logs, short_logs))


def run_backward(queries, key_rows, values, long_lengths, short_lengths, log_sums, context_grad):
    heads_here = queries.shape[1] // HEAD_DIM
    long_count = long_lengths.shape[0]
    query_long, query_short = split_buckets(queries, long_count, heads_here)
    key_long, key_short = split_buckets(key_rows, long_count, heads_here)
    value_long, value_short = split_buckets(values, long_count, heads_here)
    grad_long, grad_short = split_buckets(context_grad, long_count, heads_here)

    def one_long(entries):
        results = attend_backward(
            entries[0][None],
            entries[1][None],
            entries[2][None],
            entries[3][None],
            entries[4][None],
            entries[5][None],
        )
        return tuple((r[0] for r in results))

    long_parts = lax.map(
        one_long, (query_long, key_long, value_long, long_lengths, log_sums[0], grad_long)
    )
    short_parts = attend_backward(
        query_short, key_short, value_short, short_lengths, log_sums[1], grad_short
    )
    return tuple((join_buckets(a, b, heads_here) for a, b in zip(long_parts, short_parts)))


def grouped_product(left, right, groups):
    width = left.shape[1] // groups
    total = jnp.zeros((left.shape[0], right.shape[1]), jnp.float32)
    term = jnp.dot(
        left[:, 0 * width : 1 * width],
        right[0 * width : 1 * width],
        preferred_element_type=jnp.float32,
    )
    total = total + term.astype(jnp.bfloat16).astype(jnp.float32)
    return total


def local_layer(
    tokens,
    long_lengths,
    short_lengths,
    query_weight,
    query_bias,
    key_weight,
    value_weight,
    value_bias,
    output_weight,
    output_bias,
    first_gain,
    first_shift,
    inner_weight,
    inner_bias,
    outer_weight,
    outer_bias,
    second_gain,
    second_shift,
    out_grad,
    groups,
):
    usable = token_valid(long_lengths, short_lengths)
    query_low = (
        jnp.dot(tokens, query_weight, preferred_element_type=jnp.float32) + query_bias
    ).astype(jnp.bfloat16)
    key_low = jnp.dot(tokens, key_weight, preferred_element_type=jnp.float32).astype(jnp.bfloat16)
    value_low = (
        jnp.dot(tokens, value_weight, preferred_element_type=jnp.float32) + value_bias
    ).astype(jnp.bfloat16)
    context, log_sums = run_forward(query_low, key_low, value_low, long_lengths, short_lengths)
    context_low = context.astype(jnp.bfloat16)
    attn_part = grouped_product(context_low, output_weight, groups)
    attn_part = lax.psum(attn_part.astype(jnp.bfloat16), "tensor").astype(jnp.float32)
    attention_branch = attn_part + output_bias
    first_sum = tokens.astype(jnp.float32) + attention_branch
    first_normed, first_inverse = normalize(first_sum)
    normed = first_normed * first_gain + first_shift
    normed_low = normed.astype(jnp.bfloat16)
    inner = jnp.dot(normed_low, inner_weight, preferred_element_type=jnp.float32) + inner_bias
    active_low = jax.nn.gelu(inner, approximate=False).astype(jnp.bfloat16)
    ffn_part = grouped_product(active_low, outer_weight, groups)
    ffn_part = lax.psum(ffn_part.astype(jnp.bfloat16), "tensor").astype(jnp.float32)
    ffn_branch = ffn_part + outer_bias
    second_sum = normed + ffn_branch
    second_normed, second_inverse = normalize(second_sum)
    block_out = (second_normed * second_gain + second_shift).astype(jnp.bfloat16)
    scalars = (
        jnp.sum(usable * jnp.sum(first_sum * first_sum, axis=-1)),
        jnp.sum(usable * jnp.sum(attention_branch * attention_branch, axis=-1)),
        jnp.sum(usable * jnp.sum(ffn_branch * ffn_branch, axis=-1)),
        jnp.sum(usable),
    )
    out_cot = out_grad.astype(jnp.float32) * usable[:, None]
    second_gain_grad = jnp.sum(out_cot * second_normed, axis=0)
    second_shift_grad = jnp.sum(out_cot, axis=0)
    second_grad = norm_backward(out_cot * second_gain, second_normed, second_inverse)
    outer_bias_grad = jnp.sum(second_grad, axis=0)
    second_low = second_grad.astype(jnp.bfloat16)
    outer_weight_grad = jnp.einsum(
        "tf,td->fd", active_low, second_low, preferred_element_type=jnp.float32
    )
    active_grad = jnp.einsum(
        "td,fd->tf", second_low, outer_weight, preferred_element_type=jnp.float32
    )
    gelu_out, gelu_back = jax.vjp(lambda v: jax.nn.gelu(v, approximate=False), inner)
    inner_low = gelu_back(active_grad)[0].astype(jnp.bfloat16)
    inner_bias_grad = jnp.sum(inner_low, axis=0, dtype=jnp.float32)
    inner_weight_grad = jnp.einsum(
        "td,tf->df", normed_low, inner_low, preferred_element_type=jnp.float32
    )
    normed_part = jnp.einsum(
        "tf,df->td", inner_low, inner_weight, preferred_element_type=jnp.float32
    )
    normed_part = lax.psum(normed_part.astype(jnp.bfloat16), "tensor").astype(jnp.float32)
    normed_grad = second_grad + normed_part
    first_gain_grad = jnp.sum(normed_grad * first_normed, axis=0)
    first_shift_grad = jnp.sum(normed_grad, axis=0)
    first_grad = norm_backward(normed_grad * first_gain, first_normed, first_inverse)
    output_bias_grad = jnp.sum(first_grad, axis=0)
    first_low = first_grad.astype(jnp.bfloat16)
    output_weight_grad = jnp.einsum(
        "tc,td->cd", context_low, first_low, preferred_element_type=jnp.float32
    )
    context_grad = jnp.einsum(
        "td,cd->tc", first_low, output_weight, preferred_element_type=jnp.float32
    ).astype(jnp.bfloat16)
    query_grad, key_grad, value_grad = run_backward(
        query_low, key_low, value_low, long_lengths, short_lengths, log_sums, context_grad
    )
    query_grad = query_grad.astype(jnp.bfloat16)
    key_grad = key_grad.astype(jnp.bfloat16)
    value_grad = value_grad.astype(jnp.bfloat16)
    query_bias_grad = jnp.sum(query_grad, axis=0, dtype=jnp.float32)
    value_bias_grad = jnp.sum(value_grad, axis=0, dtype=jnp.float32)
    query_weight_grad = jnp.einsum(
        "td,tc->dc", tokens, query_grad, preferred_element_type=jnp.float32
    )
    key_weight_grad = jnp.einsum("td,tc->dc", tokens, key_grad, preferred_element_type=jnp.float32)
    value_weight_grad = jnp.einsum(
        "td,tc->dc", tokens, value_grad, preferred_element_type=jnp.float32
    )
    token_part = jnp.einsum(
        "tc,dc->td", query_grad, query_weight, preferred_element_type=jnp.float32
    )
    token_part = token_part + jnp.einsum(
        "tc,dc->td", key_grad, key_weight, preferred_element_type=jnp.float32
    )
    token_part = token_part + jnp.einsum(
        "tc,dc->td", value_grad, value_weight, preferred_element_type=jnp.float32
    )
    token_part = lax.psum(token_part.astype(jnp.bfloat16), "tensor").astype(jnp.float32)
    tokens_grad = (first_grad + token_part).astype(jnp.bfloat16)
    matrices = (
        query_weight_grad,
        key_weight_grad,
        value_weight_grad,
        inner_weight_grad,
        output_weight_grad,
        outer_weight_grad,
    )
    split_biases = (query_bias_grad, value_bias_grad, inner_bias_grad)
    shared = (
        output_bias_grad,
        first_gain_grad,
        first_shift_grad,
        outer_bias_grad,
        second_gain_grad,
        second_shift_grad,
    )
    return (block_out, tokens_grad, matrices, split_biases, shared, scalars)


def local(
    tokens,
    long_lengths,
    short_lengths,
    query_weight,
    query_bias,
    key_weight,
    value_weight,
    value_bias,
    output_weight,
    output_bias,
    first_gain,
    first_shift,
    inner_weight,
    inner_bias,
    outer_weight,
    outer_bias,
    second_gain,
    second_shift,
    out_grad,
):
    block_out, tokens_grad, matrices, split_biases, shared, scalars = local_layer(
        tokens,
        long_lengths,
        short_lengths,
        query_weight,
        query_bias,
        key_weight,
        value_weight,
        value_bias,
        output_weight,
        output_bias,
        first_gain,
        first_shift,
        inner_weight,
        inner_bias,
        outer_weight,
        outer_bias,
        second_gain,
        second_shift,
        out_grad,
        1,
    )
    resid_square, attn_square, ffn_square, token_count = scalars
    resid_square, attn_square, ffn_square, token_count = lax.psum(
        (resid_square, attn_square, ffn_square, token_count), "dp"
    )
    (
        query_weight_grad,
        key_weight_grad,
        value_weight_grad,
        inner_weight_grad,
        output_weight_grad,
        outer_weight_grad,
    ) = matrices
    (
        query_weight_grad,
        key_weight_grad,
        value_weight_grad,
        inner_weight_grad,
        output_weight_grad,
        outer_weight_grad,
    ) = (
        lax.psum_scatter(query_weight_grad, "dp", scatter_dimension=0, tiled=True),
        lax.psum_scatter(key_weight_grad, "dp", scatter_dimension=0, tiled=True),
        lax.psum_scatter(value_weight_grad, "dp", scatter_dimension=0, tiled=True),
        lax.psum_scatter(inner_weight_grad, "dp", scatter_dimension=0, tiled=True),
        lax.psum_scatter(output_weight_grad, "dp", scatter_dimension=1, tiled=True),
        lax.psum_scatter(outer_weight_grad, "dp", scatter_dimension=1, tiled=True),
    )
    query_bias_grad, value_bias_grad, inner_bias_grad = split_biases
    (
        output_bias_grad,
        first_gain_grad,
        first_shift_grad,
        outer_bias_grad,
        second_gain_grad,
        second_shift_grad,
    ) = shared
    (
        query_bias_grad,
        value_bias_grad,
        output_bias_grad,
        first_gain_grad,
        first_shift_grad,
        inner_bias_grad,
        outer_bias_grad,
        second_gain_grad,
        second_shift_grad,
    ) = lax.psum(
        (
            query_bias_grad,
            value_bias_grad,
            output_bias_grad,
            first_gain_grad,
            first_shift_grad,
            inner_bias_grad,
            outer_bias_grad,
            second_gain_grad,
            second_shift_grad,
        ),
        "dp",
    )
    denominator = token_count * D
    return (
        block_out,
        tokens_grad,
        query_weight_grad,
        query_bias_grad,
        key_weight_grad,
        value_weight_grad,
        value_bias_grad,
        output_weight_grad,
        output_bias_grad,
        first_gain_grad,
        first_shift_grad,
        inner_weight_grad,
        inner_bias_grad,
        outer_weight_grad,
        outer_bias_grad,
        second_gain_grad,
        second_shift_grad,
        jnp.sqrt(resid_square / denominator),
        jnp.sqrt(attn_square / denominator),
        jnp.sqrt(ffn_square / denominator),
    )


def solution(mesh):
    return jax.shard_map(
        local,
        mesh=mesh,
        in_specs=(
            P("dp", None),
            P("dp"),
            P("dp"),
            P(None, "tensor"),
            P("tensor"),
            P(None, "tensor"),
            P(None, "tensor"),
            P("tensor"),
            P("tensor", None),
            P(),
            P(),
            P(),
            P(None, "tensor"),
            P("tensor"),
            P("tensor", None),
            P(),
            P(),
            P(),
            P("dp", None),
        ),
        out_specs=(
            P("dp", None),
            P("dp", None),
            P("dp", "tensor"),
            P("tensor"),
            P("dp", "tensor"),
            P("dp", "tensor"),
            P("tensor"),
            P("tensor", "dp"),
            P(),
            P(),
            P(),
            P("dp", "tensor"),
            P("tensor"),
            P("tensor", "dp"),
            P(),
            P(),
            P(),
            P(),
            P(),
            P(),
        ),
        check_vma=False,
    )
```

profile of v0, /device:TPU:0, one launch (start us, length us, event | category | flops | bytes accessed | tf_op | source)
XLA Modules:
  0.0 1178.2 jit_solution(10454030748600245433)
XLA Ops:
  7.3 4.0 add_convert_fusion.5
  17.6 3.8 add_convert_fusion.4
  26.8 3.8 convolution_convert_fusion.4
  31.9 2.3 copy.113
  34.2 3.4 reshape.335
  40.7 15.8 %while.26 = (s32[]{:T(128)}, bf16[2,512,6,64]{1,3,2,0:T(8,128)(2,1)}, f32[2,6,512]{2,1,0:T(8,128)S(1)}, bf16[2,512,6,64]{1,3,2,0:T(8,128)(2,1)}, s32[2]{0:T(128)...) while((s32[]{:T(128)}, bf16[2,512,6,64]{1,3,2,0:T(8,128)(2,1)}, ...), condition=%wide.region_3.4_spmd, body=%wide.region_0.3_spmd.sunk | while | flops 421524992 | bytes 30400708 | solution.py:111
  41.9 2.6 fusion.164
  49.9 2.6 fusion.164
  59.8 2.3 copy.120
  62.2 2.6 reshape.339
  67.1 2.6 reshape.338
  69.8 2.3 copy.118
  72.1 2.8 reshape.337
  75.0 2.9 fusion.110
  82.8 3.5 convolution_convert_fusion
  86.4 26.0 %all-reduce.6.cloned.1.call-done = bf16[2048,768]{1,0:T(8,128)(2,1)} async-done(((bf16[2048,768]{1,0:T(8,128)(2,1)}), bf16[2048,768]{1,0:T(8,128)(2,1)}) %all-reduce.6.cloned.1.call-update) | async-done | bytes 3145744 | tf_op jit(solution)/shard_map/psum | solution.py:189
  112.4 4.1 fusion.67
  119.3 34.3 %multiply_convert_fusion.1 = (bf16[2048,1536]{1,0:T(8,128)(2,1)S(1)}, f32[2048,1536]{1,0:T(8,128)}, f32[2048,1536]{1,0:T(8,128)}) fusion(f32[1536]{0:T(1024)S(1)} %copy-done.70, bf16[768,1536]{1,0:T(8,128)(2,1)S(1)} %copy-done, f32[768]{0:T(1024)S(1)} %copy-done.64, f32[768]{0:T(1024)S(1)} %copy-done.48, f32[2048]{0:T(1024)S(1)} %add_rsqrt_fusion.1, ...), kind=kOutput, calls=%fused_computation.64 | convolution fusion | flops 5053612032 | bytes 40139776 | tf_op jit(solution)/shard_map/dot_general | solution.py:195
  153.6 2.7 copy-done.73
  156.3 6.4 convolution_convert_fusion.2
  163.4 23.8 %all-reduce.8.cloned.1.call-done = bf16[2048,768]{1,0:T(8,128)(2,1)} async-done(((bf16[2048,768]{1,0:T(8,128)(2,1)}), bf16[2048,768]{1,0:T(8,128)(2,1)}) %all-reduce.8.cloned.1.call-update) | async-done | bytes 3145744 | tf_op jit(solution)/shard_map/psum | solution.py:198
  187.2 6.4 fusion.103
  195.5 4.2 multiply_reduce_fusion.4
  199.7 5.0 subtract_multiply_fusion.1
  204.8 18.4 %convert_reduce_fusion = (f32[1536]{0:T(1024)}, bf16[2048,1536]{1,0:T(8,128)(2,1)}) fusion(f32[2048,1536]{1,0:T(8,128)} %get-tuple-element.295, bf16[1536,768]{1,0:T(8,128)(2,1)S(1)} %copy-done.69, f32[2048,768]{1,0:T(8,128)} %get-tuple-element.300, f32[2048,1536]{1,0:T(8,128)} %get-tuple-element.313, f32[1536]{0:T(1024)S(1)} %copy-done.70), kind=kOutput, calls=%fused_computation.62 | convolution fusion | flops 4886886912 | bytes 40120320 | tf_op jit(solution)/shard_map/td,fd->tf/dot_general | solution.py:218
  223.2 9.3 convolution_convert_fusion.1
  232.6 24.4 %all-reduce.10.cloned.1.call-done = bf16[2048,768]{1,0:T(8,128)(2,1)} async-done(((bf16[2048,768]{1,0:T(8,128)(2,1)}), bf16[2048,768]{1,0:T(8,128)(2,1)}) %all-reduce.10.cloned.1.call-update) | async-done | bytes 3145744 | tf_op jit(solution)/shard_map/psum | solution.py:230
  257.1 11.0 multiply_reduce_fusion.5
  268.0 6.3 fusion.102
  274.4 2.6 copy-done.3
  280.8 7.0 multiply_reduce_fusion.6
  287.8 6.3 multiply_convert_fusion.2
  306.5 22.6 %while.27 = (s32[]{:T(128)}, bf16[2,512,6,64]{1,3,2,0:T(8,128)(2,1)}, bf16[2,512,6,64]{1,3,2,0:T(8,128)(2,1)}, bf16[2,512,6,64]{1,3,2,0:T(8,128)(2,1)}, bf16[2,5...) while((s32[]{:T(128)}, ...), condition=%wide.region_19.20_spmd, body=%wide.region_17.19_spmd.sunk | while | flops 1030616576 | bytes 71273768 | solution.py:135
  342.0 3.6 add_convert_fusion.2
  346.0 3.3 convolution_bitcast_fusion.2
  350.7 3.9 convolution_bitcast_fusion.1
  356.1 4.1 convolution_bitcast_fusion
  361.7 6.2 fusion.72
  368.0 12.7 %fusion.88 = f32[768,1536]{1,0:T(8,128)} fusion(bf16[2048,1536]{1,0:T(8,128)(2,1)} %get-tuple-element.317, f32[768]{0:T(1024)S(1)} %copy-done.65, f32[768]{0:T(1024)S(1)} %copy-done.49, bf16[2048,768]{1,0:T(8,128)(2,1)} %all-reduce.6.cloned.1.call-done, bf16[2048,768]{1,0:T(8,128)(2,1)} %param.23, f32[2048]{0:T(1024)S(1)} %add_rsqrt_fusion.1, ...), kind=kOutput, calls=%fused_computation.144 | convolution fusion | flops 4845993984 | bytes 17327104 | tf_op jit(solution)/shard_map/td,tf->df/dot_general | solution.py:224
  381.1 10.5 fusion.75
  394.5 78.5 %all-reduce = (f32[384]{0:T(512)}, f32[384]{0:T(512)}, f32[768]{0:T(1024)}, f32[768]{0:T(1024)}, f32[768]{0:T(1024)}, /*index=5*/f32[1536]{0:T(1024)}, f32[768]{...) all-reduce(f32[384]{0:T(512)S(1)} %convert_reduce_fusion.2, ...), channel_id=1, replica_groups=mesh['dp'=16,'tensor'=2] {'dp'}, use_global_device_ids=true, to_apply=%region_24.25 | all-reduce | flops 6916 | bytes 55328 | tf_op jit(solution)/shard_map/psum | solution.py:378
  475.6 6.3 add_convert_fusion.1
  481.9 18.4 %reduce-scatter.19.cloned.1.call-done = f32[48,384]{1,0:T(8,128)} async-done(((f32[768,384]{1,0:T(8,128)}), f32[48,384]{1,0:T(8,128)}) %reduce-scatter.19.cloned.1.call-update) | async-done | bytes 73744
  500.2 127.9 %reduce-scatter.21.cloned.1.call-done = f32[48,384]{1,0:T(8,128)} async-done(((f32[768,384]{1,0:T(8,128)}), f32[48,384]{1,0:T(8,128)}) %reduce-scatter.21.cloned.1.call-update) | async-done | bytes 73744
  628.2 127.9 %reduce-scatter.23.cloned.1.call-done = f32[48,384]{1,0:T(8,128)} async-done(((f32[768,384]{1,0:T(8,128)}), f32[48,384]{1,0:T(8,128)}) %reduce-scatter.23.cloned.1.call-update) | async-done | bytes 73744
  756.1 128.0 %reduce-scatter.13.cloned.1.call-done = f32[384,48]{0,1:T(8,128)} async-done(((f32[384,768]{0,1:T(8,128)}), f32[384,48]{0,1:T(8,128)}) %reduce-scatter.13.cloned.1.call-update) | async-done | bytes 73744 | tf_op jit(solution)/shard_map/reduce_scatter | solution.py:356
  884.1 141.8 %reduce-scatter.15.cloned.1.call-done = f32[48,1536]{1,0:T(8,128)} async-done(((f32[768,1536]{1,0:T(8,128)}), f32[48,1536]{1,0:T(8,128)}) %reduce-scatter.15.cloned.1.call-update) | async-done | bytes 294928 | tf_op jit(solution)/shard_map/reduce_scatter | solution.py:355
  1025.9 141.7 %reduce-scatter.17.cloned.1.call-done = f32[1536,48]{0,1:T(8,128)} async-done(((f32[1536,768]{0,1:T(8,128)}), f32[1536,48]{0,1:T(8,128)}) %reduce-scatter.17.cloned.1.call-update) | async-done | bytes 294928 | tf_op jit(solution)/shard_map/reduce_scatter | solution.py:357
  (295 shorter events, 100.9 us)
Async XLA Ops:
  7.2 112.0 %copy-start = (bf16[768,1536]{1,0:T(8,128)(2,1)S(1)}, bf16[768,1536]{1,0:T(8,128)(2,1)}, u32[]{:S(2)}) copy-start(bf16[768,1536]{1,0:T(8,128)(2,1)} %param.35) | copy-start | bytes 7077892
  7.2 105.2 %all-reduce.6.cloned.1.call-start = ((), (), s32[]{:S(2)}) async-start(), calls=%async_computation.6 | async-start | bytes 6291456 | tf_op jit(solution)/shard_map/psum | solution.py:189
  11.3 6.3 copy-start.71
  30.6 10.1 copy-start.67
  56.5 15.6 %copy-start.8 = (bf16[2,512,6,64]{1,3,2,0:T(8,128)(2,1)}, bf16[2,512,6,64]{1,3,2,0:T(8,128)(2,1)S(1)}, u32[]{:S(2)}) copy-start(bf16[2,512,6,64]{1,3,2,0:T(8,128)(2,1)S(1)} %get-tuple-element.500) | copy-start | bytes 2359300
  56.5 15.6 %copy-start.42 = (f32[2,6,512]{2,1,0:T(8,128)}, f32[2,6,512]{2,1,0:T(8,128)S(1)}, u32[]{:S(2)}) copy-start(f32[2,6,512]{2,1,0:T(8,128)S(1)} %get-tuple-element.463) | copy-start | bytes 73732
  56.5 13.2 %copy-start.72 = (s32[4]{0:T(128)S(1)}, s32[4]{0:T(128)}, u32[]{:S(2)}) copy-start(s32[4]{0:T(128)} %param.25) | copy-start | bytes 52
  82.8 29.6 %copy-start.46 = (f32[768]{0:T(1024)S(1)}, f32[768]{0:T(1024)}, u32[]{:S(2)}) copy-start(f32[768]{0:T(1024)} %param.32) | copy-start | bytes 9220
  86.3 32.9 %copy-start.48 = (f32[768]{0:T(1024)S(1)}, f32[768]{0:T(1024)}, u32[]{:S(2)}) copy-start(f32[768]{0:T(1024)} %param.33) | copy-start | bytes 9220
  86.3 32.9 %copy-start.64 = (f32[768]{0:T(1024)S(1)}, f32[768]{0:T(1024)}, u32[]{:S(2)}) copy-start(f32[768]{0:T(1024)} %param.34) | copy-start | bytes 9220
  86.3 32.9 %copy-start.70 = (f32[1536]{0:T(1024)S(1)}, f32[1536]{0:T(1024)}, u32[]{:S(2)}) copy-start(f32[1536]{0:T(1024)} %param.36) | copy-start | bytes 18436
  86.3 100.8 %all-reduce.8.cloned.1.call-start = ((), (), s32[]{:S(2)}) async-start(), calls=%async_computation.7 | async-start | bytes 6291456 | tf_op jit(solution)/shard_map/psum | solution.py:198
  112.4 4.1 copy-start.4
  112.4 4.7 copy-start.6
  119.2 37.0 %copy-start.68 = (bf16[1536,768]{1,0:T(8,128)(2,1)S(1)}, bf16[1536,768]{1,0:T(8,128)(2,1)}, u32[]{:S(2)}) copy-start(bf16[1536,768]{1,0:T(8,128)(2,1)} %param.37) | copy-start | bytes 7077892
  156.3 30.9 %copy-start.63 = (f32[768]{0:T(1024)S(1)}, f32[768]{0:T(1024)}, u32[]{:S(2)}) copy-start(f32[768]{0:T(1024)} %param.38) | copy-start | bytes 9220
  162.6 94.4 %all-reduce.10.cloned.1.call-start = ((), (), s32[]{:S(2)}) async-start(), calls=%async_computation.8 | async-start | bytes 6291456 | tf_op jit(solution)/shard_map/psum | solution.py:230
  194.5 5.3 copy-start.66
  199.7 5.0 copy-start.69
  223.2 9.4 copy-start.41
  223.2 9.4 copy-start.45
  232.5 243.1 %all-reduce.12.cloned.1.call-start = ((), (), s32[]{:S(2)}) async-start(), calls=%async_computation.9 | async-start | bytes 6291456 | tf_op jit(solution)/shard_map/psum | solution.py:267
  257.0 11.0 copy-start.5
  257.0 11.0 copy-start.7
  257.1 11.0 copy-start.12
  268.0 9.0 copy-start.36
  280.8 16.8 %slice-start = ((s8[6291456]{0:T(1024)(128)(4,1)}), s8[4194304]{0:T(1024)(128)(4,1)S(1)}, s32[]{:S(2)}) async-start(s8[6291456]{0:T(1024)(128)(4,1)} %bitcast.212), calls=%async_computation.16 | async-start | bytes 8388608
  287.8 6.3 copy-start.16
  287.8 9.8 slice-start.1
  297.6 8.9 copy-start.9
  297.6 8.9 copy-start.10
  297.6 8.9 copy-start.15
  297.6 8.9 copy-start.43
  329.1 4.2 copy-start.37
  345.7 154.5 %reduce-scatter.19.cloned.1.call-start = ((), (), s32[]{:S(2)}) async-start(), calls=%async_computation.13 | async-start | bytes 1253376
  350.7 277.5 %reduce-scatter.21.cloned.1.call-start = ((), (), s32[]{:S(2)}) async-start(), calls=%async_computation.14 | async-start | bytes 1253376
  356.1 400.0 %reduce-scatter.23.cloned.1.call-start = ((), (), s32[]{:S(2)}) async-start(), calls=%async_computation.15 | async-start | bytes 1253376
  361.6 6.4 copy-start.47
  361.6 6.4 copy-start.49
  361.6 6.4 copy-start.65
  361.6 522.5 %reduce-scatter.13.cloned.1.call-start = ((), (), s32[]{:S(2)}) async-start(), calls=%async_computation.10 | async-start | bytes 1253376 | tf_op jit(solution)/shard_map/reduce_scatter | solution.py:356
  367.9 658.0 %reduce-scatter.15.cloned.1.call-start = ((), (), s32[]{:S(2)}) async-start(), calls=%async_computation.11 | async-start | bytes 5013504 | tf_op jit(solution)/shard_map/reduce_scatter | solution.py:355
  380.8 10.9 copy-start.50
  380.8 10.9 copy-start.51
  380.8 10.9 copy-start.52
  380.8 10.9 copy-start.61
  380.8 786.9 %reduce-scatter.17.cloned.1.call-start = ((), (), s32[]{:S(2)}) async-start(), calls=%async_computation.12 | async-start | bytes 5013504 | tf_op jit(solution)/shard_map/reduce_scatter | solution.py:357
  475.5 692.2 %copy-start.1 = (bf16[768,1536]{1,0:T(8,128)(2,1)S(1)}, bf16[768,1536]{1,0:T(8,128)(2,1)}, u32[]{:S(2)}) copy-start(bf16[768,1536]{1,0:T(8,128)(2,1)} %param.35) | copy-start | bytes 7077892
  (47 other events, 113.7 us)
Sparse Core Ops, SparseCore 0:
  86.4 25.8 all-reduce.5
  162.8 24.3 all-reduce.7
  232.6 24.3 all-reduce.9
  345.8 24.3 all-reduce.11
  375.4 124.7 reduce-scatter.18
  505.4 122.7 reduce-scatter.20
  633.5 122.5 reduce-scatter.22
  761.4 122.6 reduce-scatter.12
  889.9 136.0 reduce-scatter.14
  1032.4 135.2 reduce-scatter.16
where the time goes:
time: 1180 us
  waiting for transfers between devices  760 us (64%)
  matrix products  172 us (15%)
  blocking collectives  78.5 us (7%)
  local copies, waits for them, and re-layouts  78.3 us (7%)
  other arithmetic  66.3 us (6%)
  between operations  21.5 us (2%)
    unnamed x13, waiting for transfers between devices  274 us
    reduce_scatter x1, waiting for transfers between devices, local(): lax.psum_scatter(inner_weight_grad, 'dp', scatter_dimension=0, tiled=True)  142 us
    reduce_scatter x1, waiting for transfers between devices, local(): lax.psum_scatter(outer_weight_grad, 'dp', scatter_dimension=1, tiled=True)  142 us
    reduce_scatter x1, waiting for transfers between devices, local(): lax.psum_scatter(output_weight_grad, 'dp', scatter_dimension=1, tiled=True)  128 us
    psum x1, blocking collectives, local(): lax.psum((query_bias_grad, value_bias_grad, output_bias_grad, first_gain_...  78.5 us
    dot_general x1, matrix products, local_layer(): jnp.dot(normed_low, inner_weight, preferred_element_type=jnp.float32)  34.3 us
    psum x1, waiting for transfers between devices, local_layer(): lax.psum(attn_part.astype(jnp.bfloat16), 'tensor').astype(jnp.float32)  26 us
    psum x1, waiting for transfers between devices, local_layer(): lax.psum(normed_part.astype(jnp.bfloat16), 'tensor').astype(jnp.float32)  24.4 us
  transfers between devices with their start and end apart: 10, of which 9 were waited for; matrix products, arithmetic and copies ran while one was open for 5% of the time, Pallas kernels for 0%

commit v1 on v0

v1 whole, which is shorter than its diff:
```python
import jax
import jax.numpy as jnp
from jax import lax
from jax.experimental import pallas as pl
from jax.experimental.pallas import tpu as pltpu
from jax.sharding import PartitionSpec as P

D = 768
HEAD_DIM = 64
LONG = 512
SHORT = 256
eps_norm = 1e-05
bf = jnp.bfloat16
f32 = jnp.float32

def nt(a,b): return lax.dot_general(a,b,(((1,),(1,)),((),())),preferred_element_type=f32)
def nn(a,b): return lax.dot_general(a,b,(((1,),(0,)),((),())),preferred_element_type=f32)
def tn(a,b): return lax.dot_general(a,b,(((0,),(0,)),((),())),preferred_element_type=f32)

def fwd_seq(lens_ref, idx, q_ref,k_ref,v_ref,ctx_ref,linv_ref,e_ref, row, size, e_at):
    rows=pl.ds(row,size)
    lane=lax.broadcasted_iota(jnp.int32,(size,128),1)
    low=lane<64
    pos=lax.broadcasted_iota(jnp.int32,(size,128),0)
    bias=jnp.where(pos<lens_ref[idx],0.0,-1e30).astype(bf)
    q=q_ref[rows,:]*jnp.asarray(0.125,bf); k=k_ref[rows,:]; v=v_ref[rows,:]
    one=jnp.ones((),bf); zero=jnp.zeros((),bf)
    outs=[]
    for h in range(2):
        mine=low if h==0 else ~low
        flag=lane==(64 if h==0 else 0)
        qh=jnp.where(mine,q,jnp.where(flag,one,zero))
        kh=jnp.where(mine,k,jnp.where(flag,bias,zero))
        vh=jnp.where(mine,v,one)
        s=nt(qh,kh)
        m=jnp.max(s,axis=-1,keepdims=True)
        e=jnp.exp(s-m).astype(bf)
        e_ref[e_at(h)]=e
        outs.append(nn(e,vh))
    num=jnp.where(low,outs[0],outs[1])
    den=pltpu.roll(jnp.where(low,outs[1],outs[0]),64,1)
    inv=1.0/den
    linv_ref[rows,:]=inv
    ctx_ref[rows,:]=(num*inv).astype(bf)

def fwd_kernel(lens_ref,q_ref,k_ref,v_ref,ctx_ref,linv_ref,el_ref,es_ref):
    fwd_seq(lens_ref,0,q_ref,k_ref,v_ref,ctx_ref,linv_ref,el_ref,0,LONG,lambda h:(0,h))
    for s in range(2):
        fwd_seq(lens_ref,1+s,q_ref,k_ref,v_ref,ctx_ref,linv_ref,es_ref,LONG+s*SHORT,SHORT,lambda h,s=s:(0,2*s+h))

def attend_fwd(lens,q,k,v):
    pairs=q.shape[1]//128
    T=q.shape[0]
    col=pl.BlockSpec((T,128),lambda i,*_:(0,i))
    return pl.pallas_call(fwd_kernel,
        out_shape=(jax.ShapeDtypeStruct(q.shape,bf),jax.ShapeDtypeStruct(q.shape,f32),
                   jax.ShapeDtypeStruct((pairs,2,LONG,LONG),bf),jax.ShapeDtypeStruct((pairs,4,SHORT,SHORT),bf)),
        grid_spec=pltpu.PrefetchScalarGridSpec(num_scalar_prefetch=1,grid=(pairs,),
            in_specs=[col,col,col],
            out_specs=[col,col,pl.BlockSpec((1,2,LONG,LONG),lambda i,*_:(i,0,0,0)),pl.BlockSpec((1,4,SHORT,SHORT),lambda i,*_:(i,0,0,0))]),
        compiler_params=pltpu.CompilerParams(vmem_limit_bytes=48<<20),
        cost_estimate=pl.CostEstimate(flops=int(3e9),bytes_accessed=int(10e6),transcendentals=int(2.4e6)),
        name="attend_fwd")(lens,q,k,v)

def bwd_seq(q_ref,k_ref,v_ref,ctx_ref,linv_ref,g_ref,e_ref,dq_ref,dk_ref,dv_ref,row,size,e_at):
    rows=pl.ds(row,size)
    lane=lax.broadcasted_iota(jnp.int32,(size,128),1)
    low=lane<64
    q=q_ref[rows,:]*jnp.asarray(0.125,bf); k=k_ref[rows,:]*jnp.asarray(0.125,bf); v=v_ref[rows,:]
    g=g_ref[rows,:].astype(f32)*linv_ref[rows,:]
    prod=g*ctx_ref[rows,:].astype(f32)
    gl=g.astype(bf)
    one=jnp.ones((),bf); zero=jnp.zeros((),bf)
    dqs=[];dks=[];dvs=[]
    for h in range(2):
        mine=low if h==0 else ~low
        base=64 if h==0 else 0
        delta=-jnp.sum(jnp.where(mine,prod,0.0),axis=-1,keepdims=True)
        hi=delta.astype(bf); lo=(delta-hi.astype(f32)).astype(bf)
        gh=jnp.where(mine,gl,jnp.where(lane==base,hi,jnp.where(lane==base+1,lo,zero)))
        vh=jnp.where(mine,v,one)
        e=e_ref[e_at(h)]
        dp=nt(gh,vh)
        ds=(e.astype(f32)*dp).astype(bf)
        dqs.append(nn(ds,k))
        dks.append(tn(ds,q))
        dvs.append(tn(e,gl))
    dq_ref[rows,:]=jnp.where(low,dqs[0],dqs[1]).astype(bf)
    dk_ref[rows,:]=jnp.where(low,dks[0],dks[1]).astype(bf)
    dv_ref[rows,:]=jnp.where(low,dvs[0],dvs[1]).astype(bf)

def bwd_kernel(q_ref,k_ref,v_ref,ctx_ref,linv_ref,g_ref,el_ref,es_ref,dq_ref,dk_ref,dv_ref):
    bwd_seq(q_ref,k_ref,v_ref,ctx_ref,linv_ref,g_ref,el_ref,dq_ref,dk_ref,dv_ref,0,LONG,lambda h:(0,h))
    for s in range(2):
        bwd_seq(q_ref,k_ref,v_ref,ctx_ref,linv_ref,g_ref,es_ref,dq_ref,dk_ref,dv_ref,LONG+s*SHORT,SHORT,lambda h,s=s:(0,2*s+h))

def attend_bwd(q,k,v,ctx,linv,g,el,es):
    pairs=q.shape[1]//128
    T=q.shape[0]
    col=pl.BlockSpec((T,128),lambda i:(0,i))
    return pl.pallas_call(bwd_kernel,
        out_shape=(jax.ShapeDtypeStruct(q.shape,bf),)*3,
        grid=(pairs,),
        in_specs=[col]*6+[pl.BlockSpec((1,2,LONG,LONG),lambda i:(i,0,0,0)),pl.BlockSpec((1,4,SHORT,SHORT),lambda i:(i,0,0,0))],
        out_specs=[col]*3,
        compiler_params=pltpu.CompilerParams(vmem_limit_bytes=48<<20),
        cost_estimate=pl.CostEstimate(flops=int(6e9),bytes_accessed=int(10e6),transcendentals=0),
        name="attend_bwd")(q,k,v,ctx,linv,g,el,es)

def normalize(values):
    centered = values - jnp.mean(values, axis=-1, keepdims=True)
    inverse_dev = lax.rsqrt(jnp.mean(centered * centered, axis=-1, keepdims=True) + eps_norm)
    return (centered * inverse_dev, inverse_dev)


def norm_backward(scaled, normed, inverse_dev):
    centred_grad = scaled - jnp.mean(scaled, axis=-1, keepdims=True)
    return inverse_dev * (centred_grad - normed * jnp.mean(scaled * normed, axis=-1, keepdims=True))


def swap_tensor(value):
    return lax.ppermute(value, "tensor", [(0, 1), (1, 0)])


def dp_bits():
    count = lax.axis_size("dp")
    bits = []
    while (1 << len(bits)) < count:
        bits.append(1 << len(bits))
    return count, bits


def swap_dp(value, bit):
    count, _ = dp_bits()
    return lax.ppermute(value, "dp", [(i, i ^ bit) for i in range(count)])


def scatter_rows(total, order):
    count, bits = dp_bits()
    rows = total.shape[0] // count
    index = lax.axis_index("dp")
    names = list(reversed(bits))
    view = total.reshape([2] * len(names) + [rows, total.shape[1]])
    for step, bit in enumerate(order):
        axis = names.index(bit)
        mine = (index // bit) % 2
        send = lax.dynamic_index_in_dim(view, 1 - mine, axis, keepdims=False)
        keep = lax.dynamic_index_in_dim(view, mine, axis, keepdims=False)
        view = keep.astype(f32) + swap_dp(send, bit).astype(f32)
        if step < len(order) - 1:
            view = view.astype(bf)
        names.pop(axis)
    return view


def sum_dp(value):
    _, bits = dp_bits()
    for bit in bits:
        value = value + swap_dp(value, bit)
    return value


def rows_here(array, side):
    half = array.shape[0] // 4
    first = lax.dynamic_slice_in_dim(array, side * half, half, 0)
    second = lax.dynamic_slice_in_dim(array, 2 * half + side * half, half, 0)
    return jnp.concatenate([first, second], 0)


def rows_joined(own, other, side):
    half = own.shape[0] // 2
    zero = side == 0
    low, high = (jnp.where(zero, own, other), jnp.where(zero, other, own))
    return jnp.concatenate([low[:half], high[:half], low[half:], high[half:]], 0)


def dot(left, right):
    return jnp.dot(left, right, preferred_element_type=f32)


def dot_nt(left, right):
    return lax.dot_general(left, right, (((1,), (1,)), ((), ())), preferred_element_type=f32)


def dot_tn(left, right):
    return lax.dot_general(left, right, (((0,), (0,)), ((), ())), preferred_element_type=f32)


def local(
    tokens,
    long_lengths,
    short_lengths,
    query_weight,
    query_bias,
    key_weight,
    value_weight,
    value_bias,
    output_weight,
    output_bias,
    first_gain,
    first_shift,
    inner_weight,
    inner_bias,
    outer_weight,
    outer_bias,
    second_gain,
    second_shift,
    out_grad,
):
    side = lax.axis_index("tensor")
    _, bits = dp_bits()
    alternate = bits[1::-1] + bits[2:]
    nl, ns = (long_lengths.shape[0] // 2, short_lengths.shape[0] // 2)
    lens = jnp.concatenate(
        [
            lax.dynamic_slice_in_dim(long_lengths, side * nl, nl),
            lax.dynamic_slice_in_dim(short_lengths, side * ns, ns),
        ]
    )
    qkv_own = jnp.concatenate([query_weight, key_weight, value_weight], 1)
    qkv_other = swap_tensor(qkv_own)
    biases = jnp.concatenate([query_bias, value_bias, inner_bias])
    biases_other = swap_tensor(biases)
    width = query_weight.shape[1]
    output_other = swap_tensor(output_weight)
    inner_other = swap_tensor(inner_weight)
    outer_other = swap_tensor(outer_weight)
    qkv_w = (qkv_own, qkv_other)
    out_w = (output_weight, output_other)
    in_w = (inner_weight, inner_other)
    outer_w = (outer_weight, outer_other)
    bias_q = (query_bias, biases_other[:width])
    bias_v = (value_bias, biases_other[width : 2 * width])
    bias_i = (inner_bias, biases_other[2 * width :])

    x = rows_here(tokens, side)
    xf = x.astype(f32)
    usable = jnp.concatenate(
        [
            (jnp.arange(size, dtype=jnp.int32) < lens[i]).astype(f32)
            for i, size in enumerate([LONG] * nl + [SHORT] * ns)
        ]
    )
    out_cot = rows_here(out_grad, side).astype(f32) * usable[:, None]

    saved = []
    branch = output_bias
    for h in range(2):
        packed = dot(x, qkv_w[h])
        q = (packed[:, :width] + bias_q[h]).astype(bf)
        k = packed[:, width : 2 * width].astype(bf)
        v = (packed[:, 2 * width :] + bias_v[h]).astype(bf)
        ctx, linv, e_long, e_short = attend_fwd(lens, q, k, v)
        saved.append((q, k, v, ctx, linv, e_long, e_short))
        branch = branch + dot(ctx, out_w[h])
    first_sum = xf + branch
    first_normed, first_inverse = normalize(first_sum)
    normed = first_normed * first_gain + first_shift
    normed_low = normed.astype(bf)
    active, slope = ([], [])
    ffn = outer_bias
    for h in range(2):
        inner = dot(normed_low, in_w[h]) + bias_i[h]
        phi = 0.5 * (1.0 + lax.erf(inner * 0.7071067811865476))
        active.append((inner * phi).astype(bf))
        slope.append((phi + inner * (0.3989422804014327 * jnp.exp(-0.5 * inner * inner))).astype(bf))
        ffn = ffn + dot(active[h], outer_w[h])
    second_sum = normed + ffn
    second_normed, second_inverse = normalize(second_sum)
    block_own = (second_normed * second_gain + second_shift).astype(bf)
    block_other = swap_tensor(block_own)
    block_out = rows_joined(block_own, block_other, side)
    squares = [jnp.sum(usable[:, None] * a * a) for a in (first_sum, branch, ffn)]

    second_grad = norm_backward(out_cot * second_gain, second_normed, second_inverse)
    second_low = second_grad.astype(bf)
    outer_part = dot_tn(second_low, active[1]).astype(bf)
    outer_part = dot_tn(second_low, active[0]) + swap_tensor(outer_part).astype(f32)
    outer_rows = scatter_rows(outer_part.astype(bf), bits)
    inner_low = [
        (dot_nt(second_low, outer_w[h]) * slope[h].astype(f32)).astype(bf) for h in range(2)
    ]
    inner_part = dot_tn(normed_low, inner_low[1]).astype(bf)
    inner_part = dot_tn(normed_low, inner_low[0]) + swap_tensor(inner_part).astype(f32)
    inner_rows = scatter_rows(inner_part.astype(bf), alternate)
    normed_grad = second_grad
    for h in range(2):
        normed_grad = normed_grad + dot_nt(inner_low[h], in_w[h])
    first_grad = norm_backward(normed_grad * first_gain, first_normed, first_inverse)
    first_low = first_grad.astype(bf)
    shared = jnp.stack(
        [
            jnp.sum(first_grad, axis=0),
            jnp.sum(normed_grad * first_normed, axis=0),
            jnp.sum(normed_grad, axis=0),
            jnp.sum(second_grad, axis=0),
            jnp.sum(out_cot * second_normed, axis=0),
            jnp.sum(out_cot, axis=0),
            jnp.pad(jnp.stack(squares + [jnp.sum(lens).astype(f32)]), (0, D - 4)),
        ]
    )
    inner_sums = [jnp.sum(inner_low[h], axis=0, dtype=f32).reshape(-1, D) for h in range(2)]
    early = jnp.concatenate([shared, inner_sums[0]]) + swap_tensor(
        jnp.concatenate([shared, inner_sums[1]])
    )
    early = sum_dp(early)

    grads = []
    qkvo = [None, None]
    tokens_part = first_grad
    qv_sums = [None, None]
    for h in (1, 0):
        q, k, v, ctx, linv, e_long, e_short = saved[h]
        context_grad = dot_nt(first_low, out_w[h]).astype(bf)
        dq, dk, dv = attend_bwd(q, k, v, ctx, linv, context_grad, e_long, e_short)
        packed = jnp.concatenate([dq, dk, dv], 1)
        qv_sums[h] = jnp.concatenate([jnp.sum(dq, axis=0, dtype=f32), jnp.sum(dv, axis=0, dtype=f32)])
        qkvo[h] = (dot_tn(x, packed), dot_tn(first_low, ctx))
        tokens_part = tokens_part + dot_nt(packed, qkv_w[h])
    sent = swap_tensor(jnp.concatenate([a.astype(bf) for a in qkvo[1]], 1)).astype(f32)
    qkvo_part = (jnp.concatenate(qkvo[0], 1) + sent).astype(bf)
    half = 2 * width
    first_half = scatter_rows(qkvo_part[:, :half], bits)
    second_half = scatter_rows(qkvo_part[:, half:], alternate)
    late = sum_dp(qv_sums[0] + swap_tensor(qv_sums[1]))
    tokens_own = tokens_part.astype(bf)
    tokens_grad = rows_joined(tokens_own, swap_tensor(tokens_own), side)

    rms = jnp.sqrt(early[6, :3] / (early[6, 3] * D))
    return (
        block_out,
        tokens_grad,
        first_half[:, :width],
        late[:width],
        first_half[:, width:],
        second_half[:, :width],
        late[width:],
        second_half[:, width:].T,
        early[0],
        early[1],
        early[2],
        inner_rows,
        early[7:].reshape(-1),
        outer_rows.T,
        early[3],
        early[4],
        early[5],
        rms[0],
        rms[1],
        rms[2],
    )


def solution(mesh):
    return jax.shard_map(
        local,
        mesh=mesh,
        in_specs=(
            P("dp", None),
            P("dp"),
            P("dp"),
            P(None, "tensor"),
            P("tensor"),
            P(None, "tensor"),
            P(None, "tensor"),
            P("tensor"),
            P("tensor", None),
            P(),
            P(),
            P(),
            P(None, "tensor"),
            P("tensor"),
            P("tensor", None),
            P(),
            P(),
            P(),
            P("dp", None),
        ),
        out_specs=(
            P("dp", None),
            P("dp", None),
            P("dp", "tensor"),
            P("tensor"),
            P("dp", "tensor"),
            P("dp", "tensor"),
            P("tensor"),
            P("tensor", "dp"),
            P(),
            P(),
            P(),
            P("dp", "tensor"),
            P("tensor"),
            P("tensor", "dp"),
            P(),
            P(),
            P(),
            P(),
            P(),
            P(),
        ),
        check_vma=False,
    )
```

time: 1180 us -> 305 us (0.26)
  waiting for transfers between devices: 760 us -> 70.3 us
  blocking collectives: 78.5 us -> 0 us
  matrix products: 172 us -> 99.6 us
  local copies, waits for them, and re-layouts: 78.3 us -> 26.1 us
  starting transfers between devices: 0.88 us -> 37.5 us
  other arithmetic: 66.3 us -> 31.2 us
  Pallas kernels: 0 us -> 33 us
  between operations: 21.5 us -> 3.97 us
    reduce_scatter x3 -> x0, waiting for transfers between devices: 412 us -> none  [the longest x1 142 us: local(): lax.psum_scatter(inner_weight_grad, 'dp', scatter_dimension=0, tiled=True)]
    unnamed x13 -> x0, waiting for transfers between devices: 274 us -> none
    psum x1 -> x0, blocking collectives: 78.5 us -> none  [local(): lax.psum((query_bias_grad, value_bias_grad, output_bias_grad, first_gain_...]
    psum x4 -> x0, waiting for transfers between devices: 74.2 us -> none  [the longest x1 26 us: local_layer(): lax.psum(attn_part.astype(jnp.bfloat16), 'tensor').astype(jnp.float32)]
    dot_general x38 -> x24, matrix products: 172 us -> 99.6 us  [the longest x8 38.1 us: dot_nt(): lax.dot_general(left, right, (((1,), (1,)), ((), ())), preferred_element_...]
    ppermute x0 -> x36, waiting for transfers between devices: none -> 70.3 us  [the longest x24 70.3 us: swap_dp(): return lax.ppermute(value, 'dp', [(i, i ^ bit) for i in range(count)])]
    ppermute x0 -> x36, starting transfers between devices: none -> 37.5 us  [the longest x24 34.5 us: swap_dp(): return lax.ppermute(value, 'dp', [(i, i ^ bit) for i in range(count)])]
    pallas_call x0 -> x4, Pallas kernels: none -> 33 us  [the longest x2 19.5 us: attend_bwd(): pl.pallas_call(bwd_kernel, out_shape=(jax.ShapeDtypeStruct(q.shape, bf),)...]
  transfers between devices with their start and end apart: 10 -> 36, of which waited for: 9 -> 14; matrix products, arithmetic and copies ran while one was open for 5% -> 29% of each run, Pallas kernels for 0% -> 8%
where the time goes in v1:
time: 305 us; the launch traced here: 302 us
  matrix products  99.6 us (33%)
  waiting for transfers between devices  70.3 us (23%)
  starting transfers between devices  37.5 us (12%)
  Pallas kernels  33 us (11%)
  other arithmetic  31.2 us (10%)
  local copies, waits for them, and re-layouts  26.1 us (9%)
  between operations  3.97 us (1%)
    ppermute x24, waiting for transfers between devices, swap_dp(): return lax.ppermute(value, 'dp', [(i, i ^ bit) for i in range(count)])  70.3 us
    dot_general x8, matrix products, dot_nt(): lax.dot_general(left, right, (((1,), (1,)), ((), ())), preferred_element_...  38.1 us
    ppermute x24, starting transfers between devices, swap_dp(): return lax.ppermute(value, 'dp', [(i, i ^ bit) for i in range(count)])  34.5 us
    dot_general x8, matrix products, dot(): return jnp.dot(left, right, preferred_element_type=f32)  32.4 us
    dot_general x8, matrix products, dot_tn(): lax.dot_general(left, right, (((0,), (0,)), ((), ())), preferred_element_...  29.2 us
    pallas_call x2, Pallas kernels, attend_bwd(): pl.pallas_call(bwd_kernel, out_shape=(jax.ShapeDtypeStruct(q.shape, bf),)...  19.5 us
    unnamed x112, local copies, waits for them, and re-layouts  13.5 us
    pallas_call x2, Pallas kernels, attend_fwd(): pl.pallas_call(fwd_kernel, out_shape=(jax.ShapeDtypeStruct(q.shape, bf),...  13.4 us
  transfers between devices with their start and end apart: 36, of which 14 were waited for; matrix products, arithmetic and copies ran while one was open for 29% of the time, Pallas kernels for 8%

profile of v1, /device:TPU:0, one launch (start us, length us, event | category | flops | bytes accessed | tf_op | source)
XLA Modules:
  0.0 301.7 jit_solution(17691647067786743558)
XLA Ops:
  0.7 2.2 constant_dynamic-update-slice_fusion.2
  9.8 4.3 %fusion.39 = f32[1024,1152]{1,0:T(8,128)S(1)} fusion(bf16[768,1152]{1,0:T(8,128)(2,1)} %constant_dynamic-update-slice_fusion, bf16[512,768]{1,0:T(8,128)(2,1)S(1)} %get-tuple-element.91, bf16[512,768]{1,0:T(8,128)(2,1)S(1)} %get-tuple-element.90), kind=kOutput, calls=%fused_computation.184 | convolution fusion | flops 1815085056 | bytes 8060928 | tf_op jit(solution)/shard_map/dot_general | solution.py:178
  19.2 6.8 %attend_fwd.2 = (bf16[1024,384]{1,0:T(8,128)(2,1)S(1)}, f32[1024,384]{1,0:T(8,128)S(1)}, bf16[3,2,512,512]{3,2,1,0:T(8,128)(2,1)}, bf16[3,4,256,256]{3,2,1,0:T(8,128)(2,1)}) custom-call(s32[3]{0:T(128)S(1)} %pad_add_fusion.lens_ref, bf16[1024,384]{1,0:T(8,128)(2,1)S(1)} %get-tuple-element.82.q_ref, bf16[1024,384]{1,0:T(8,128)(2,1)S(1)} %slice.218.k_ref, ...), custom_call_target="tpu_custom_call" | custom-call | flops 3000000000 | bytes 10000000 | tf_op jit(solution)/shard_map/attend_fwd/pallas_call | solution.py:55
  27.2 2.6 fusion.56
  31.2 3.9 %fusion.38 = f32[1024,1152]{1,0:T(8,128)S(1)} fusion(bf16[768,1152]{1,0:T(8,128)(2,1)} %collective-permute-done, bf16[512,768]{1,0:T(8,128)(2,1)} %copy-done.17, bf16[512,768]{1,0:T(8,128)(2,1)S(1)} %copy-done.15), kind=kOutput, calls=%fused_computation.183 | convolution fusion | flops 1815085056 | bytes 8060928 | tf_op jit(solution)/shard_map/dot_general | solution.py:178
  35.5 6.6 %attend_fwd.3 = (bf16[1024,384]{1,0:T(8,128)(2,1)S(1)}, f32[1024,384]{1,0:T(8,128)S(1)}, bf16[3,2,512,512]{3,2,1,0:T(8,128)(2,1)}, bf16[3,4,256,256]{3,2,1,0:T(8,128)(2,1)}) custom-call(s32[3]{0:T(128)S(1)} %pad_add_fusion.lens_ref, bf16[1024,384]{1,0:T(8,128)(2,1)S(1)} %get-tuple-element.80.q_ref, bf16[1024,384]{1,0:T(8,128)(2,1)S(1)} %slice.217.k_ref, ...), custom_call_target="tpu_custom_call" | custom-call | flops 3000000000 | bytes 10000000 | tf_op jit(solution)/shard_map/attend_fwd/pallas_call | solution.py:55
  42.2 2.7 fusion.45
  47.2 4.9 %multiply_convert_fusion.3 = (bf16[1024,1536]{1,0:T(8,128)(2,1)S(1)}, f32[1024,1536]{1,0:T(8,128)}) fusion(f32[1536]{0:T(1024)S(1)} %copy-done.39, bf16[1024,768]{1,0:T(8,128)(2,1)S(1)} %fusion.18, bf16[768,1536]{1,0:T(8,128)(2,1)S(1)} %copy-done.45), kind=kOutput, calls=%fused_computation.18 | convolution fusion | flops 2425356288 | bytes 13375488 | tf_op jit(solution)/shard_map/dot_general | solution.py:178
  52.1 2.6 fusion.57
  54.8 6.4 %multiply_convert_fusion.2 = (bf16[1024,1536]{1,0:T(8,128)(2,1)S(1)}, f32[1024,1536]{1,0:T(8,128)}) fusion(f32[1536]{0:T(1024)S(1)} %slice.169, bf16[1024,768]{1,0:T(8,128)(2,1)S(1)} %fusion.18, bf16[768,1536]{1,0:T(8,128)(2,1)} %collective-permute-done.3), kind=kOutput, calls=%fused_computation.16 | convolution fusion | flops 2425356288 | bytes 13375488 | tf_op jit(solution)/shard_map/dot_general | solution.py:178
  61.2 4.8 %fusion.43 = (f32[1024]{0:T(1024)S(1)}, f32[1024,768]{1,0:T(8,128)S(1)}, f32[1024,768]{1,0:T(8,128)S(1)}) fusion(f32[768]{0:T(1024)S(1)} %copy-done.41, f32[768]{0:T(1024)S(1)} %copy-done.36, f32[1024]{0:T(1024)S(1)} %add_rsqrt_fusion.1, f32[1024,768]{1,0:T(8,128)S(1)} %get-tuple-element.78, f32[1024]{0:T(1024)S(1)} %broadcast_multiply_fusion.5, ...), kind=kOutput, calls=%fused_computation.188 | convolution fusion | flops 2422209536 | bytes 18109440 | tf_op jit(solution)/shard_map/dot_general | solution.py:178
  67.4 4.1 %fusion.12 = (f32[]{:T(128)}, f32[]{:T(128)}, f32[768]{0:T(1024)S(1)}, f32[1024]{0:T(1024)S(1)}, f32[1024]{0:T(1024)S(1)}, /*index=5*/f32[768]{0:T(1024)S(1)}) fusion(f32[1024,768]{1,0:T(8,128)S(1)} %get-tuple-element.123, f32[1024]{0:T(1024)S(1)} %add_convert_fusion.4, f32[1024,768]{1,0:T(8,128)S(1)} %get-tuple-element.128, ...), kind=kLoop, calls=%fused_computation.31 | loop fusion | flops 15725054 | bytes 11039752 | tf_op jit(solution)/shard_map/reduce_sum | solution.py:273
  71.5 3.0 %fusion.41 = (f32[768]{0:T(1024)S(1)}, f32[1024,768]{1,0:T(8,128)S(1)}, bf16[1024,768]{1,0:T(8,128)(2,1)}) fusion(f32[1024]{0:T(1024)S(1)} %broadcast_multiply_fusion.2, f32[1024,768]{1,0:T(8,128)S(1)} %get-tuple-element.76, f32[1024]{0:T(1024)S(1)} %broadcast_multiply_fusion.4, f32[1024]{0:T(1024)S(1)} %broadcast_multiply_fusion.3, f32[768]{0:T(1024)S(1)} %copy-done.35, ...), kind=kLoop, calls=%fused_computation.186 | loop fusion | flops 12582144 | bytes 9466880 | tf_op jit(solution)/shard_map/reduce_sum | solution.py:296
  74.7 4.0 %convolution_convert_fusion = bf16[768,1536]{1,0:T(8,128)(2,1)} fusion(bf16[1024,768]{1,0:T(8,128)(2,1)S(1)} %convert_element_type.311, bf16[1024,1536]{1,0:T(8,128)(2,1)S(1)} %get-tuple-element.126), kind=kOutput, calls=%fused_computation.27 | convolution fusion | flops 2417098752 | bytes 7077888 | tf_op jit(solution)/shard_map/dot_general | solution.py:186
  78.8 6.6 %convert_reduce_fusion.1 = (f32[1536]{0:T(1024)S(1)}, bf16[1024,1536]{1,0:T(8,128)(2,1)}) fusion(f32[1024,1536]{1,0:T(8,128)S(1)} %bitcast.164, f32[1536]{0:T(1024)S(1)} %copy-done.39, bf16[1024,768]{1,0:T(8,128)(2,1)S(1)} %convert_element_type.311, bf16[1536,768]{1,0:T(8,128)(2,1)S(1)} %copy-done.44), kind=kOutput, calls=%fused_computation.13 | convolution fusion | flops 2439510528 | bytes 13381632 | tf_op jit(solution)/shard_map/dot_general | solution.py:182
  85.4 4.5 %fusion.58 = f32[1024,768]{1,0:T(8,128)S(1)} fusion(bf16[1024,1536]{1,0:T(8,128)(2,1)} %get-tuple-element.131, bf16[768,1536]{1,0:T(8,128)(2,1)S(1)} %copy-done.45), kind=kOutput, calls=%fused_computation.202 | convolution fusion | flops 2415919104 | bytes 8650752 | tf_op jit(solution)/shard_map/dot_general | solution.py:182
  89.9 7.0 %convert_reduce_fusion = (f32[1536]{0:T(1024)S(1)}, bf16[1024,1536]{1,0:T(8,128)(2,1)S(1)}) fusion(f32[1024,1536]{1,0:T(8,128)} %get-tuple-element.127, f32[1536]{0:T(1024)S(1)} %slice.169, bf16[1024,768]{1,0:T(8,128)(2,1)S(1)} %convert_element_type.311, bf16[1536,768]{1,0:T(8,128)(2,1)} %collective-permute-done.4), kind=kOutput, calls=%fused_computation.12 | convolution fusion | flops 2439510528 | bytes 13381632 | tf_op jit(solution)/shard_map/dot_general | solution.py:182
  96.9 4.4 %convolution_convert_fusion.1 = bf16[768,1536]{1,0:T(8,128)(2,1)} fusion(bf16[1024,768]{1,0:T(8,128)(2,1)S(1)} %fusion.18, bf16[1024,1536]{1,0:T(8,128)(2,1)S(1)} %get-tuple-element.133), kind=kOutput, calls=%fused_computation.28 | convolution fusion | flops 2417098752 | bytes 7077888 | tf_op jit(solution)/shard_map/dot_general | solution.py:186
  101.3 6.4 %multiply_reduce_fusion.1 = (f32[768]{0:T(1024)S(1)}, f32[1024]{0:T(1024)S(1)}, f32[1024]{0:T(1024)S(1)}, f32[]{:T(128)}, f32[768]{0:T(1024)S(1)}, /*index=5*/f32[1024,768]{1,0:T(8,128)S(1)}) fusion(f32[1024,768]{1,0:T(8,128)S(1)} %get-tuple-element.78, f32[1024]{0:T(1024)S(1)} %add_rsqrt_fusion.1, f32[1024]{0:T(1024)S(1)} %broadcast_multiply_fusion.5, ...), kind=kOutput, calls=%fused_computation.36 | convolution fusion | flops 2426925568 | bytes 18117636 | tf_op jit(solution)/shard_map/dot_general | solution.py:182
  112.1 3.0 convolution_convert_fusion.4.g_ref
  115.1 9.8 %attend_bwd.2 = (bf16[1024,384]{1,0:T(8,128)(2,1)S(1)}, bf16[1024,384]{1,0:T(8,128)(2,1)S(1)}, bf16[1024,384]{1,0:T(8,128)(2,1)S(1)}) custom-call(bf16[1024,384]{1,0:T(8,128)(2,1)S(1)} %get-tuple-element.80.q_ref, bf16[1024,384]{1,0:T(8,128)(2,1)S(1)} %slice.217.k_ref, bf16[1024,384]{1,0:T(8,128)(2,1)S(1)} %get-tuple-element.79.v_ref, ...), custom_call_target="tpu_custom_call" | custom-call | flops 6000000000 | bytes 10000000 | tf_op jit(solution)/shard_map/attend_bwd/pallas_call | solution.py:101
  126.0 2.0 select_maximum_fusion
  130.7 5.3 %convolution_convert_fusion.2 = bf16[768,1152]{1,0:T(8,128)(2,1)} fusion(bf16[1024,1152]{1,0:T(8,128)(2,1)} %constant_dynamic-update-slice_fusion.3, bf16[512,768]{1,0:T(8,128)(2,1)S(1)} %copy-done.19, bf16[512,768]{1,0:T(8,128)(2,1)S(1)} %copy-done.16), kind=kOutput, calls=%fused_computation.29 | convolution fusion | flops 1815969792 | bytes 5701632 | tf_op jit(solution)/shard_map/dot_general | solution.py:186
  136.0 9.8 %attend_bwd.3 = (bf16[1024,384]{1,0:T(8,128)(2,1)S(1)}, bf16[1024,384]{1,0:T(8,128)(2,1)S(1)}, bf16[1024,384]{1,0:T(8,128)(2,1)S(1)}) custom-call(bf16[1024,384]{1,0:T(8,128)(2,1)S(1)} %copy-done.3, bf16[1024,384]{1,0:T(8,128)(2,1)S(1)} %slice.218.k_ref, bf16[1024,384]{1,0:T(8,128)(2,1)S(1)} %copy-done.1, bf16[1024,384]{1,0:T(8,128)(2,1)S(1)} %get-tuple-element.34.ctx_ref, ...), custom_call_target="tpu_custom_call" | custom-call | flops 6000000000 | bytes 10000000 | tf_op jit(solution)/shard_map/attend_bwd/pallas_call | solution.py:101
  146.9 4.0 %fusion.59 = f32[1024,768]{1,0:T(8,128)S(1)} fusion(bf16[1024,1152]{1,0:T(8,128)(2,1)S(1)} %constant_dynamic-update-slice_fusion.6, bf16[768,1152]{1,0:T(8,128)(2,1)} %constant_dynamic-update-slice_fusion), kind=kOutput, calls=%fused_computation.203 | convolution fusion | flops 1811939328 | bytes 7274496 | tf_op jit(solution)/shard_map/dot_general | solution.py:182
  150.9 4.9 %add_convert_fusion.2 = bf16[1024,768]{1,0:T(8,128)(2,1)} fusion(f32[1024,768]{1,0:T(8,128)S(1)} %fusion.59, f32[1024,768]{1,0:T(8,128)S(1)} %copy-done.11, bf16[1024,1152]{1,0:T(8,128)(2,1)S(1)} %copy-done.34, bf16[768,1152]{1,0:T(8,128)(2,1)} %collective-permute-done), kind=kOutput, calls=%fused_computation.37 | convolution fusion | flops 1814298624 | bytes 11993088 | tf_op jit(solution)/shard_map/dot_general | solution.py:182
  155.9 2.5 collective-permute-start.13
  158.5 4.0 %fusion.37 = f32[768,1152]{1,0:T(8,128)} fusion(bf16[1024,1152]{1,0:T(8,128)(2,1)S(1)} %constant_dynamic-update-slice_fusion.6, bf16[512,768]{1,0:T(8,128)(2,1)S(1)} %copy-done.19, bf16[512,768]{1,0:T(8,128)(2,1)S(1)} %copy-done.16), kind=kOutput, calls=%fused_computation.182 | convolution fusion | flops 1815085056 | bytes 7471104 | tf_op jit(solution)/shard_map/dot_general | solution.py:186
  165.3 2.0 fusion.60
  171.5 2.6 collective-permute-start.16
  180.6 2.8 collective-permute-done.25
  186.5 2.1 broadcast_select_fusion.1
  196.0 4.2 %add_convert_fusion = bf16[768,1536]{1,0:T(8,128)(2,1)S(1)} fusion(bf16[768,1536]{1,0:T(8,128)(2,1)} %collective-permute-done.31, bf16[1024,768]{1,0:T(8,128)(2,1)S(1)} %copy-done.25, bf16[1024,1536]{1,0:T(8,128)(2,1)S(1)} %copy-done.49), kind=kOutput, calls=%fused_computation.25 | convolution fusion | flops 2419458048 | bytes 9437184 | tf_op jit(solution)/shard_map/dot_general | solution.py:186
  202.6 2.2 fusion.10
  208.4 4.2 %add_convert_fusion.1 = bf16[768,1536]{1,0:T(8,128)(2,1)S(1)} fusion(bf16[768,1536]{1,0:T(8,128)(2,1)} %collective-permute-done.26, bf16[1024,768]{1,0:T(8,128)(2,1)S(1)} %copy-done.23, bf16[1024,1536]{1,0:T(8,128)(2,1)S(1)} %copy-done.50), kind=kOutput, calls=%fused_computation.26 | convolution fusion | flops 2419458048 | bytes 9437184 | tf_op jit(solution)/shard_map/dot_general | solution.py:186
  213.0 8.3 %collective-permute-done.17 = bf16[2,2,2,48,768]{4,3,0,1,2:T(8,128)(2,1)S(1)} collective-permute-done((bf16[2,2,2,48,768]{4,3,0,1,2:T(8,128)(2,1)S(1)}, bf16[2,2,2,48,768]{4,3,0,1,2:T(8,128)(2,1)S(1)}, u32[]{:S(2)}, u32[]{:S(2)}) %collective-permute-start.17) | collective-permute-done | bytes 589856 | tf_op jit(solution)/shard_map/ppermute | solution.py:135
  222.7 19.3 %collective-permute-done.8 = bf16[2,2,2,48,768]{4,3,0,1,2:T(8,128)(2,1)S(1)} collective-permute-done((bf16[2,2,2,48,768]{4,3,0,1,2:T(8,128)(2,1)S(1)}, bf16[2,2,2,48,768]{4,3,0,1,2:T(8,128)(2,1)S(1)}, u32[]{:S(2)}, u32[]{:S(2)}) %collective-permute-start.8) | collective-permute-done | bytes 589856 | tf_op jit(solution)/shard_map/ppermute | solution.py:135
  243.5 4.5 %collective-permute-done.18 = bf16[2,2,48,768]{3,2,0,1:T(8,128)(2,1)S(1)} collective-permute-done((bf16[2,2,48,768]{3,2,0,1:T(8,128)(2,1)S(1)}, bf16[2,2,48,768]{3,2,0,1:T(8,128)(2,1)S(1)}, u32[]{:S(2)}, u32[]{:S(2)}) %collective-permute-start.18) | collective-permute-done | bytes 294944 | tf_op jit(solution)/shard_map/ppermute | solution.py:135
  249.2 3.3 %collective-permute-done.9 = bf16[2,2,48,768]{3,2,0,1:T(8,128)(2,1)S(1)} collective-permute-done((bf16[2,2,48,768]{3,2,0,1:T(8,128)(2,1)S(1)}, bf16[2,2,48,768]{3,2,0,1:T(8,128)(2,1)S(1)}, u32[]{:S(2)}, u32[]{:S(2)}) %collective-permute-start.9) | collective-permute-done | bytes 294944 | tf_op jit(solution)/shard_map/ppermute | solution.py:135
  253.8 2.5 collective-permute-start.20
  256.3 3.2 %collective-permute-done.10 = bf16[2,48,768]{2,1,0:T(8,128)(2,1)S(1)} collective-permute-done((bf16[2,48,768]{2,1,0:T(8,128)(2,1)S(1)}, bf16[2,48,768]{2,1,0:T(8,128)(2,1)S(1)}, u32[]{:S(2)}, u32[]{:S(2)}) %collective-permute-start.10) | collective-permute-done | bytes 147488 | tf_op jit(solution)/shard_map/ppermute | solution.py:135
  261.5 4.1 %collective-permute-done.11 = bf16[48,768]{1,0:T(8,128)(2,1)S(1)} collective-permute-done((bf16[48,768]{1,0:T(8,128)(2,1)S(1)}, bf16[48,768]{1,0:T(8,128)(2,1)S(1)}, u32[]{:S(2)}, u32[]{:S(2)}) %collective-permute-start.11) | collective-permute-done | bytes 73760 | tf_op jit(solution)/shard_map/ppermute | solution.py:135
  269.4 8.5 %collective-permute-done.33 = bf16[2,2,48,1536]{3,2,0,1:T(8,128)(2,1)S(1)} collective-permute-done((bf16[2,2,48,1536]{3,2,0,1:T(8,128)(2,1)S(1)}, bf16[2,2,48,1536]{3,2,0,1:T(8,128)(2,1)S(1)}, u32[]{:S(2)}, u32[]{:S(2)}) %collective-permute-start.33) | collective-permute-done | bytes 589856 | tf_op jit(solution)/shard_map/ppermute | solution.py:135
  280.6 7.5 %collective-permute-done.34 = bf16[2,48,1536]{2,1,0:T(8,128)(2,1)S(1)} collective-permute-done((bf16[2,48,1536]{2,1,0:T(8,128)(2,1)S(1)}, bf16[2,48,1536]{2,1,0:T(8,128)(2,1)S(1)}, u32[]{:S(2)}, u32[]{:S(2)}) %collective-permute-start.34) | collective-permute-done | bytes 294944 | tf_op jit(solution)/shard_map/ppermute | solution.py:135
  288.2 2.1 collective-permute-start.35
  290.3 2.6 collective-permute-done.29
  293.0 2.3 collective-permute-start.30
  297.5 3.2 %collective-permute-done.30 = bf16[48,1536]{1,0:T(8,128)(2,1)S(1)} collective-permute-done((bf16[48,1536]{1,0:T(8,128)(2,1)S(1)}, bf16[48,1536]{1,0:T(8,128)(2,1)S(1)}, u32[]{:S(2)}, u32[]{:S(2)}) %collective-permute-start.30) | collective-permute-done | bytes 147488 | tf_op jit(solution)/shard_map/ppermute | solution.py:135
  (283 shorter events, 73.0 us)
Async XLA Ops:
  0.7 7.7 %copy-start.43 = (s32[4]{0:T(128)S(1)}, s32[4]{0:T(128)}, u32[]{:S(2)}) copy-start(s32[4]{0:T(128)} %param.21) | copy-start | bytes 52
  0.7 8.4 %copy-start.47 = (s32[2]{0:T(128)S(1)}, s32[2]{0:T(128)}, u32[]{:S(2)}) copy-start(s32[2]{0:T(128)} %param.20) | copy-start | bytes 28
  0.7 9.0 %copy-start.30 = (bf16[2048,768]{1,0:T(8,128)(2,1)S(1)}, bf16[2048,768]{1,0:T(8,128)(2,1)}, u32[]{:S(2)}) copy-start(bf16[2048,768]{1,0:T(8,128)(2,1)} %param.19) | copy-start | bytes 9437188
  6.9 24.3 %collective-permute-start = (bf16[768,1152]{1,0:T(8,128)(2,1)}, bf16[768,1152]{1,0:T(8,128)(2,1)}, u32[]{:S(2)}, u32[]{:S(2)}) collective-permute-start(bf16[768,1152]{1,0:T(8,128)(2,1)} %constant_dynamic-update-slice_fusion), channel_id=1, source_target_pairs={{0,1},{1,0},{2,3},{3,2},{4,5},{5,4},{6,7},{7,6},{8,9},{9,8},{10,11... | collective-permute-start | bytes 5308424 | tf_op jit(solution)/shard_map/ppermute | solution.py:122
  7.3 23.8 %collective-permute-start.1 = (f32[2304]{0:T(1024)S(1)}, f32[2304]{0:T(1024)S(1)}, u32[]{:S(2)}, u32[]{:S(2)}) collective-permute-start(f32[2304]{0:T(1024)S(1)} %pad_maximum_fusion.5), channel_id=1, source_target_pairs={{0,1},{1,0},{2,3},{3,2},{4,5},{5,4},{6,7},{7,6},{8,9},{9,8},{10,11... | collective-permute-start | bytes 27656 | tf_op jit(solution)/shard_map/ppermute | solution.py:122
  7.4 34.7 %collective-permute-start.2 = (bf16[384,768]{1,0:T(8,128)(2,1)}, bf16[384,768]{1,0:T(8,128)(2,1)}, u32[]{:S(2)}, u32[]{:S(2)}) collective-permute-start(bf16[384,768]{1,0:T(8,128)(2,1)} %param.27), channel_id=1, source_target_pairs={{0,1},{1,0},{2,3},{3,2},{4,5},{5,4},{6,7},{7,6},{8,9},{9,8},{10,11... | collective-permute-start | bytes 1769480 | tf_op jit(solution)/shard_map/ppermute | solution.py:122
  7.9 46.8 %collective-permute-start.3 = (bf16[768,1536]{1,0:T(8,128)(2,1)}, bf16[768,1536]{1,0:T(8,128)(2,1)}, u32[]{:S(2)}, u32[]{:S(2)}) collective-permute-start(bf16[768,1536]{1,0:T(8,128)(2,1)} %param.31), channel_id=1, source_target_pairs={{0,1},{1,0},{2,3},{3,2},{4,5},{5,4},{6,7},{7,6},{8,9},{9,8},{10,11... | collective-permute-start | bytes 7077896 | tf_op jit(solution)/shard_map/ppermute | solution.py:122
  8.0 53.2 %collective-permute-start.4 = (bf16[1536,768]{1,0:T(8,128)(2,1)}, bf16[1536,768]{1,0:T(8,128)(2,1)}, u32[]{:S(2)}, u32[]{:S(2)}) collective-permute-start(bf16[1536,768]{1,0:T(8,128)(2,1)} %param.33), channel_id=1, source_target_pairs={{0,1},{1,0},{2,3},{3,2},{4,5},{5,4},{6,7},{7,6},{8,9},{9,8},{10,11... | collective-permute-start | bytes 7077896 | tf_op jit(solution)/shard_map/ppermute | solution.py:122
  9.8 9.4 %copy-start.17 = (bf16[512,768]{1,0:T(8,128)(2,1)}, bf16[512,768]{1,0:T(8,128)(2,1)S(1)}, u32[]{:S(2)}) copy-start(bf16[512,768]{1,0:T(8,128)(2,1)S(1)} %get-tuple-element.91) | copy-start | bytes 2359300
  9.8 7.7 %copy-start.31 = (bf16[2048,768]{1,0:T(8,128)(2,1)S(1)}, bf16[2048,768]{1,0:T(8,128)(2,1)}, u32[]{:S(2)}) copy-start(bf16[2048,768]{1,0:T(8,128)(2,1)} %param.37) | copy-start | bytes 9437188
  19.2 8.0 %copy-start.32 = (bf16[384,768]{1,0:T(8,128)(2,1)S(1)}, bf16[384,768]{1,0:T(8,128)(2,1)}, u32[]{:S(2)}) copy-start(bf16[384,768]{1,0:T(8,128)(2,1)} %param.27) | copy-start | bytes 1769476
  42.1 72.9 %copy-start.4 = (bf16[1024,384]{1,0:T(8,128)(2,1)}, bf16[1024,384]{1,0:T(8,128)(2,1)S(1)}, u32[]{:S(2)}) copy-start(bf16[1024,384]{1,0:T(8,128)(2,1)S(1)} %get-tuple-element.35.ctx_ref) | copy-start | bytes 2359300
  47.2 49.7 %copy-start.22 = (bf16[1024,768]{1,0:T(8,128)(2,1)}, bf16[1024,768]{1,0:T(8,128)(2,1)S(1)}, u32[]{:S(2)}) copy-start(bf16[1024,768]{1,0:T(8,128)(2,1)S(1)} %fusion.18) | copy-start | bytes 4718596
  74.7 15.2 %copy-start.24 = (bf16[1024,768]{1,0:T(8,128)(2,1)}, bf16[1024,768]{1,0:T(8,128)(2,1)S(1)}, u32[]{:S(2)}) copy-start(bf16[1024,768]{1,0:T(8,128)(2,1)S(1)} %convert_element_type.311) | copy-start | bytes 4718596
  128.5 36.2 %collective-permute-start.21 = (f32[9,768]{1,0:T(8,128)S(1)}, f32[9,768]{1,0:T(8,128)S(1)}, u32[]{:S(2)}, u32[]{:S(2)}) collective-permute-start(f32[9,768]{1,0:T(8,128)S(1)} %concatenate.69), channel_id=1, source_target_pairs={{0,1},{1,0},{2,3},{3,2},{4,5},{5,4},{6,7},{7,6},{8,9},{9,8},{10,11... | collective-permute-start | bytes 82952 | tf_op jit(solution)/shard_map/ppermute | solution.py:122
  146.4 9.5 %collective-permute-start.12 = (f32[768]{0:T(1024)S(1)}, f32[768]{0:T(1024)S(1)}, u32[]{:S(2)}, u32[]{:S(2)}) collective-permute-start(f32[768]{0:T(1024)S(1)} %pad_maximum_fusion.6), channel_id=1, source_target_pairs={{0,1},{1,0},{2,3},{3,2},{4,5},{5,4},{6,7},{7,6},{8,9},{9,8},{10,11... | collective-permute-start | bytes 9224 | tf_op jit(solution)/shard_map/ppermute | solution.py:122
  155.9 9.4 %copy-start.27 = (bf16[1024,768]{1,0:T(8,128)(2,1)S(1)}, bf16[1024,768]{1,0:T(8,128)(2,1)}, u32[]{:S(2)}) copy-start(bf16[1024,768]{1,0:T(8,128)(2,1)} %copy-done.26) | copy-start | bytes 4718596
  155.9 7.2 %collective-permute-start.13 = (f32[768]{0:T(1024)S(1)}, f32[768]{0:T(1024)S(1)}, u32[]{:S(2)}, u32[]{:S(2)}) collective-permute-start(f32[768]{0:T(1024)S(1)} %maximum_add_fusion.1), channel_id=1, source_target_pairs={{0,2},{2,0},{4,6},{6,4},{8,10},{10,8},{12,14},{14,12},{16,18},{18,... | collective-permute-start | bytes 9224 | tf_op jit(solution)/shard_map/ppermute | solution.py:135
  162.4 7.5 %copy-start.5 = (bf16[1024,384]{1,0:T(8,128)(2,1)S(1)}, bf16[1024,384]{1,0:T(8,128)(2,1)}, u32[]{:S(2)}) copy-start(bf16[1024,384]{1,0:T(8,128)(2,1)} %copy-done.4) | copy-start | bytes 2359300
  162.8 23.7 %collective-permute-start.6 = (bf16[1024,768]{1,0:T(8,128)(2,1)}, bf16[1024,768]{1,0:T(8,128)(2,1)}, u32[]{:S(2)}, u32[]{:S(2)}) collective-permute-start(bf16[1024,768]{1,0:T(8,128)(2,1)} %add_convert_fusion.2), channel_id=1, source_target_pairs={{0,1},{1,0},{2,3},{3,2},{4,5},{5,4},{6,7},{7,6},{8,9},{9,8},{10,11... | collective-permute-start | bytes 4718600 | tf_op jit(solution)/shard_map/ppermute | solution.py:122
  163.1 4.2 %collective-permute-start.14 = (f32[768]{0:T(1024)S(1)}, f32[768]{0:T(1024)S(1)}, u32[]{:S(2)}, u32[]{:S(2)}) collective-permute-start(f32[768]{0:T(1024)S(1)} %add.389), channel_id=1, source_target_pairs={{0,4},{2,6},{4,0},{6,2},{8,12},{10,14},{12,8},{14,10},{16,20},{18,... | collective-permute-start | bytes 9224 | tf_op jit(solution)/shard_map/ppermute | solution.py:135
  164.7 4.3 %collective-permute-start.22 = (f32[9,768]{1,0:T(8,128)S(1)}, f32[9,768]{1,0:T(8,128)S(1)}, u32[]{:S(2)}, u32[]{:S(2)}) collective-permute-start(f32[9,768]{1,0:T(8,128)S(1)} %add.397), channel_id=1, source_target_pairs={{0,2},{2,0},{4,6},{6,4},{8,10},{10,8},{12,14},{14,12},{16,18},{18,... | collective-permute-start | bytes 82952 | tf_op jit(solution)/shard_map/ppermute | solution.py:135
  167.3 7.9 %copy-start.21 = (bf16[768,1152]{1,0:T(8,128)(2,1)S(1)}, bf16[768,1152]{1,0:T(8,128)(2,1)}, u32[]{:S(2)}) copy-start(bf16[768,1152]{1,0:T(8,128)(2,1)} %convolution_convert_fusion.2) | copy-start | bytes 5308420
  167.3 4.2 %collective-permute-start.15 = (f32[768]{0:T(1024)S(1)}, f32[768]{0:T(1024)S(1)}, u32[]{:S(2)}, u32[]{:S(2)}) collective-permute-start(f32[768]{0:T(1024)S(1)} %add.390), channel_id=1, source_target_pairs={{0,8},{2,10},{4,12},{6,14},{8,0},{10,2},{12,4},{14,6},{16,24},{18,... | collective-permute-start | bytes 9224 | tf_op jit(solution)/shard_map/ppermute | solution.py:135
  169.0 5.1 %collective-permute-start.23 = (f32[9,768]{1,0:T(8,128)S(1)}, f32[9,768]{1,0:T(8,128)S(1)}, u32[]{:S(2)}, u32[]{:S(2)}) collective-permute-start(f32[9,768]{1,0:T(8,128)S(1)} %add.398), channel_id=1, source_target_pairs={{0,4},{2,6},{4,0},{6,2},{8,12},{10,14},{12,8},{14,10},{16,20},{18,... | collective-permute-start | bytes 82952 | tf_op jit(solution)/shard_map/ppermute | solution.py:135
  170.9 23.4 %collective-permute-start.31 = (bf16[768,1536]{1,0:T(8,128)(2,1)}, bf16[768,1536]{1,0:T(8,128)(2,1)}, u32[]{:S(2)}, u32[]{:S(2)}) collective-permute-start(bf16[768,1536]{1,0:T(8,128)(2,1)} %convolution_convert_fusion), channel_id=1, source_target_pairs={{0,1},{1,0},{2,3},{3,2},{4,5},{5,4},{6,7},{7,6},{8,9},{9,8},{10,11... | collective-permute-start | bytes 7077896 | tf_op jit(solution)/shard_map/ppermute | solution.py:122
  171.0 17.7 %collective-permute-start.5 = (bf16[1024,768]{1,0:T(8,128)(2,1)S(1)}, bf16[1024,768]{1,0:T(8,128)(2,1)}, u32[]{:S(2)}, u32[]{:S(2)}) collective-permute-start(bf16[1024,768]{1,0:T(8,128)(2,1)S(1)} %copy-done.20), channel_id=1, source_target_pairs={{0,1},{1,0},{2,3},{3,2},{4,5},{5,4},{6,7},{7,6},{8,9},{9,8},{10,11... | collective-permute-start | bytes 4718600 | tf_op jit(solution)/shard_map/ppermute | solution.py:122
  171.5 5.4 %collective-permute-start.16 = (f32[768]{0:T(1024)S(1)}, f32[768]{0:T(1024)S(1)}, u32[]{:S(2)}, u32[]{:S(2)}) collective-permute-start(f32[768]{0:T(1024)S(1)} %add.391), channel_id=1, source_target_pairs={{0,16},{2,18},{4,20},{6,22},{8,24},{10,26},{12,28},{14,30},{16,0},... | collective-permute-start | bytes 9224 | tf_op jit(solution)/shard_map/ppermute | solution.py:135
  174.2 4.2 %collective-permute-start.24 = (f32[9,768]{1,0:T(8,128)S(1)}, f32[9,768]{1,0:T(8,128)S(1)}, u32[]{:S(2)}, u32[]{:S(2)}) collective-permute-start(f32[9,768]{1,0:T(8,128)S(1)} %add.399), channel_id=1, source_target_pairs={{0,8},{2,10},{4,12},{6,14},{8,0},{10,2},{12,4},{14,6},{16,24},{18,... | collective-permute-start | bytes 82952 | tf_op jit(solution)/shard_map/ppermute | solution.py:135
  177.0 31.4 %collective-permute-start.26 = (bf16[768,1536]{1,0:T(8,128)(2,1)}, bf16[768,1536]{1,0:T(8,128)(2,1)}, u32[]{:S(2)}, u32[]{:S(2)}) collective-permute-start(bf16[768,1536]{1,0:T(8,128)(2,1)} %convolution_convert_fusion.1), channel_id=1, source_target_pairs={{0,1},{1,0},{2,3},{3,2},{4,5},{5,4},{6,7},{7,6},{8,9},{9,8},{10,11... | collective-permute-start | bytes 7077896 | tf_op jit(solution)/shard_map/ppermute | solution.py:122
  178.3 5.1 %collective-permute-start.25 = (f32[9,768]{1,0:T(8,128)S(1)}, f32[9,768]{1,0:T(8,128)S(1)}, u32[]{:S(2)}, u32[]{:S(2)}) collective-permute-start(f32[9,768]{1,0:T(8,128)S(1)} %add.400), channel_id=1, source_target_pairs={{0,16},{2,18},{4,20},{6,22},{8,24},{10,26},{12,28},{14,30},{16,0},... | collective-permute-start | bytes 82952 | tf_op jit(solution)/shard_map/ppermute | solution.py:135
  183.4 18.3 %collective-permute-start.7 = (bf16[768,1536]{1,0:T(8,128)(2,1)}, bf16[768,1536]{1,0:T(8,128)(2,1)}, u32[]{:S(2)}, u32[]{:S(2)}) collective-permute-start(bf16[768,1536]{1,0:T(8,128)(2,1)} %pad_maximum_fusion.2), channel_id=1, source_target_pairs={{0,1},{1,0},{2,3},{3,2},{4,5},{5,4},{6,7},{7,6},{8,9},{9,8},{10,11... | collective-permute-start | bytes 7077896 | tf_op jit(solution)/shard_map/ppermute | solution.py:122
  200.5 65.8 %collective-permute-start.32 = (bf16[2,2,2,48,1536]{4,3,0,1,2:T(8,128)(2,1)S(1)}, bf16[2,2,2,48,1536]{4,3,0,1,2:T(8,128)(2,1)S(1)}, u32[]{:S(2)}, u32[]{:S(2)}) collective-permute-start(bf16[2,2,2,48,1536]{4,3,0,1,2:T(8,128)(2,1)S(1)} %bitcast.159), channel_id=1, source_target_pairs={{0,2},{2,0},{4,6},{6,4},{8,10},{10,8},{12,14},{14,12},{16,18},{18,... | collective-permute-start | bytes 3538952 | tf_op jit(solution)/shard_map/ppermute | solution.py:135
  205.1 16.2 %collective-permute-start.17 = (bf16[2,2,2,48,768]{4,3,0,1,2:T(8,128)(2,1)S(1)}, bf16[2,2,2,48,768]{4,3,0,1,2:T(8,128)(2,1)S(1)}, u32[]{:S(2)}, u32[]{:S(2)}) collective-permute-start(bf16[2,2,2,48,768]{4,3,0,1,2:T(8,128)(2,1)S(1)} %bitcast.162), channel_id=1, source_target_pairs={{0,4},{2,6},{4,0},{6,2},{8,12},{10,14},{12,8},{14,10},{16,20},{18,... | collective-permute-start | bytes 1769480 | tf_op jit(solution)/shard_map/ppermute | solution.py:135
  206.4 35.6 %collective-permute-start.8 = (bf16[2,2,2,48,768]{4,3,0,1,2:T(8,128)(2,1)S(1)}, bf16[2,2,2,48,768]{4,3,0,1,2:T(8,128)(2,1)S(1)}, u32[]{:S(2)}, u32[]{:S(2)}) collective-permute-start(bf16[2,2,2,48,768]{4,3,0,1,2:T(8,128)(2,1)S(1)} %bitcast.161), channel_id=1, source_target_pairs={{0,2},{2,0},{4,6},{6,4},{8,10},{10,8},{12,14},{14,12},{16,18},{18,... | collective-permute-start | bytes 1769480 | tf_op jit(solution)/shard_map/ppermute | solution.py:135
  212.9 54.7 %collective-permute-start.27 = (bf16[2,2,2,48,1536]{4,3,0,1,2:T(8,128)(2,1)S(1)}, bf16[2,2,2,48,1536]{4,3,0,1,2:T(8,128)(2,1)S(1)}, u32[]{:S(2)}, u32[]{:S(2)}) collective-permute-start(bf16[2,2,2,48,1536]{4,3,0,1,2:T(8,128)(2,1)S(1)} %bitcast.160), channel_id=1, source_target_pairs={{0,4},{2,6},{4,0},{6,2},{8,12},{10,14},{12,8},{14,10},{16,20},{18,... | collective-permute-start | bytes 3538952 | tf_op jit(solution)/shard_map/ppermute | solution.py:135
  221.5 26.5 %collective-permute-start.18 = (bf16[2,2,48,768]{3,2,0,1:T(8,128)(2,1)S(1)}, bf16[2,2,48,768]{3,2,0,1:T(8,128)(2,1)S(1)}, u32[]{:S(2)}, u32[]{:S(2)}) collective-permute-start(bf16[2,2,48,768]{3,2,0,1:T(8,128)(2,1)S(1)} %dynamic-slice_bitcast_fusion.4), channel_id=1, source_target_pairs={{0,2},{2,0},{4,6},{6,4},{8,10},{10,8},{12,14},{14,12},{16,18},{18,... | collective-permute-start | bytes 884744 | tf_op jit(solution)/shard_map/ppermute | solution.py:135
  242.2 10.3 %collective-permute-start.9 = (bf16[2,2,48,768]{3,2,0,1:T(8,128)(2,1)S(1)}, bf16[2,2,48,768]{3,2,0,1:T(8,128)(2,1)S(1)}, u32[]{:S(2)}, u32[]{:S(2)}) collective-permute-start(bf16[2,2,48,768]{3,2,0,1:T(8,128)(2,1)S(1)} %dynamic-slice_bitcast_fusion.5), channel_id=1, source_target_pairs={{0,4},{2,6},{4,0},{6,2},{8,12},{10,14},{12,8},{14,10},{16,20},{18,... | collective-permute-start | bytes 884744 | tf_op jit(solution)/shard_map/ppermute | solution.py:135
  248.1 5.7 %collective-permute-start.19 = (bf16[2,48,768]{2,1,0:T(8,128)(2,1)S(1)}, bf16[2,48,768]{2,1,0:T(8,128)(2,1)S(1)}, u32[]{:S(2)}, u32[]{:S(2)}) collective-permute-start(bf16[2,48,768]{2,1,0:T(8,128)(2,1)S(1)} %dynamic-slice_bitcast_fusion.8), channel_id=1, source_target_pairs={{0,8},{2,10},{4,12},{6,14},{8,0},{10,2},{12,4},{14,6},{16,24},{18,... | collective-permute-start | bytes 442376 | tf_op jit(solution)/shard_map/ppermute | solution.py:135
  252.6 6.9 %collective-permute-start.10 = (bf16[2,48,768]{2,1,0:T(8,128)(2,1)S(1)}, bf16[2,48,768]{2,1,0:T(8,128)(2,1)S(1)}, u32[]{:S(2)}, u32[]{:S(2)}) collective-permute-start(bf16[2,48,768]{2,1,0:T(8,128)(2,1)S(1)} %dynamic-slice_bitcast_fusion.9), channel_id=1, source_target_pairs={{0,8},{2,10},{4,12},{6,14},{8,0},{10,2},{12,4},{14,6},{16,24},{18,... | collective-permute-start | bytes 442376 | tf_op jit(solution)/shard_map/ppermute | solution.py:135
  253.8 7.1 %collective-permute-start.20 = (bf16[48,768]{1,0:T(8,128)(2,1)S(1)}, bf16[48,768]{1,0:T(8,128)(2,1)S(1)}, u32[]{:S(2)}, u32[]{:S(2)}) collective-permute-start(bf16[48,768]{1,0:T(8,128)(2,1)S(1)} %dynamic-slice_bitcast_fusion.10), channel_id=1, source_target_pairs={{0,16},{2,18},{4,20},{6,22},{8,24},{10,26},{12,28},{14,30},{16,0},... | collective-permute-start | bytes 221192 | tf_op jit(solution)/shard_map/ppermute | solution.py:135
  259.6 6.1 %collective-permute-start.11 = (bf16[48,768]{1,0:T(8,128)(2,1)S(1)}, bf16[48,768]{1,0:T(8,128)(2,1)S(1)}, u32[]{:S(2)}, u32[]{:S(2)}) collective-permute-start(bf16[48,768]{1,0:T(8,128)(2,1)S(1)} %dynamic-slice_bitcast_fusion.11), channel_id=1, source_target_pairs={{0,16},{2,18},{4,20},{6,22},{8,24},{10,26},{12,28},{14,30},{16,0},... | collective-permute-start | bytes 221192 | tf_op jit(solution)/shard_map/ppermute | solution.py:135
  266.7 11.2 %collective-permute-start.33 = (bf16[2,2,48,1536]{3,2,0,1:T(8,128)(2,1)S(1)}, bf16[2,2,48,1536]{3,2,0,1:T(8,128)(2,1)S(1)}, u32[]{:S(2)}, u32[]{:S(2)}) collective-permute-start(bf16[2,2,48,1536]{3,2,0,1:T(8,128)(2,1)S(1)} %dynamic-slice_bitcast_fusion), channel_id=1, source_target_pairs={{0,4},{2,6},{4,0},{6,2},{8,12},{10,14},{12,8},{14,10},{16,20},{18,... | collective-permute-start | bytes 1769480 | tf_op jit(solution)/shard_map/ppermute | solution.py:135
  267.9 11.9 %collective-permute-start.28 = (bf16[2,2,48,1536]{3,2,0,1:T(8,128)(2,1)S(1)}, bf16[2,2,48,1536]{3,2,0,1:T(8,128)(2,1)S(1)}, u32[]{:S(2)}, u32[]{:S(2)}) collective-permute-start(bf16[2,2,48,1536]{3,2,0,1:T(8,128)(2,1)S(1)} %dynamic-slice_bitcast_fusion.1), channel_id=1, source_target_pairs={{0,2},{2,0},{4,6},{6,4},{8,10},{10,8},{12,14},{14,12},{16,18},{18,... | collective-permute-start | bytes 1769480 | tf_op jit(solution)/shard_map/ppermute | solution.py:135
  278.1 10.0 %collective-permute-start.34 = (bf16[2,48,1536]{2,1,0:T(8,128)(2,1)S(1)}, bf16[2,48,1536]{2,1,0:T(8,128)(2,1)S(1)}, u32[]{:S(2)}, u32[]{:S(2)}) collective-permute-start(bf16[2,48,1536]{2,1,0:T(8,128)(2,1)S(1)} %dynamic-slice_bitcast_fusion.2), channel_id=1, source_target_pairs={{0,8},{2,10},{4,12},{6,14},{8,0},{10,2},{12,4},{14,6},{16,24},{18,... | collective-permute-start | bytes 884744 | tf_op jit(solution)/shard_map/ppermute | solution.py:135
  280.1 12.8 %collective-permute-start.29 = (bf16[2,48,1536]{2,1,0:T(8,128)(2,1)S(1)}, bf16[2,48,1536]{2,1,0:T(8,128)(2,1)S(1)}, u32[]{:S(2)}, u32[]{:S(2)}) collective-permute-start(bf16[2,48,1536]{2,1,0:T(8,128)(2,1)S(1)} %dynamic-slice_bitcast_fusion.3), channel_id=1, source_target_pairs={{0,8},{2,10},{4,12},{6,14},{8,0},{10,2},{12,4},{14,6},{16,24},{18,... | collective-permute-start | bytes 884744 | tf_op jit(solution)/shard_map/ppermute | solution.py:135
  288.2 8.6 %collective-permute-start.35 = (bf16[48,1536]{1,0:T(8,128)(2,1)S(1)}, bf16[48,1536]{1,0:T(8,128)(2,1)S(1)}, u32[]{:S(2)}, u32[]{:S(2)}) collective-permute-start(bf16[48,1536]{1,0:T(8,128)(2,1)S(1)} %dynamic-slice_bitcast_fusion.6), channel_id=1, source_target_pairs={{0,16},{2,18},{4,20},{6,22},{8,24},{10,26},{12,28},{14,30},{16,0},... | collective-permute-start | bytes 442376 | tf_op jit(solution)/shard_map/ppermute | solution.py:135
  293.0 7.7 %collective-permute-start.30 = (bf16[48,1536]{1,0:T(8,128)(2,1)S(1)}, bf16[48,1536]{1,0:T(8,128)(2,1)S(1)}, u32[]{:S(2)}, u32[]{:S(2)}) collective-permute-start(bf16[48,1536]{1,0:T(8,128)(2,1)S(1)} %dynamic-slice_bitcast_fusion.7), channel_id=1, source_target_pairs={{0,16},{2,18},{4,20},{6,22},{8,24},{10,26},{12,28},{14,30},{16,0},... | collective-permute-start | bytes 442376 | tf_op jit(solution)/shard_map/ppermute | solution.py:135
  (41 other events, 160.7 us)
